TPU v7x, 128 devices: a whole 4x4x4 slice. The times are simulated.
128 devices in a mesh: lat: 4 (over z_lo, core), lon: 32 (over x, z_hi, y).
Axes of the slice: x: 4, y: 4, z: 4 (z_hi: 2, z_lo: 2; z = z_hi * 2 + z_lo), core: 2. Of those that a mesh axis runs over, the one named last changes fastest.
Arguments:
- cell_state: bfloat16 [4, 32, 512, 32, 64], P('lat', 'lon'), may hold values from -6 to 6
- remap_weight: bfloat16 [4, 32, 512, 64, 128], P('lat', 'lon'), may hold values from -0.75 to 0.75
- block_target: int32 [4, 32, 512], P('lat', 'lon'), may hold values from 0 to 255, as said below
- block_count: int32 [4, 32], P('lat', 'lon'), may hold values from 256 to 512, as said below
- border_state: bfloat16 [4, 32, 128, 32, 64], P('lat', 'lon'), may hold values from -6 to 6
- border_weight: bfloat16 [4, 32, 128, 64, 128], P('lat', 'lon'), may hold values from -0.75 to 0.75
- border_target: int32 [4, 32, 128], P('lat', 'lon'), may hold values from 0 to 63
- kernel_one: bfloat16 [7, 7, 32, 64], replicated, may hold values from -0.15625 to 0.15625
- bias_one: float32 [64], replicated, may hold values from -4 to 4
- gain_one: float32 [64], replicated, may hold values from 0.1 to 1.9
- kernel_two: bfloat16 [7, 7, 64, 128], replicated, may hold values from -0.109375 to 0.109375
- bias_two: float32 [128], replicated, may hold values from -4 to 4
- gain_two: float32 [128], replicated, may hold values from 0.1 to 1.9
Outputs:
- encoded: bfloat16 [256, 1024, 128], P('lat', 'lon')
Inputs may be any that keep to these rules, and one draw needn't show every extreme that they name: `block_count`: slots below a device's count are live; the largest count is exactly 512 in every draw. `block_target`: on every device, slots 0 to 255 name each patch of the tile once, in an order drawn from the seed; later slots name patches at random.
All inputs are finite; a program needn't handle non-finite values.
Results may differ from a plain program's by a relative error of at most 0.0045.
Values may be sent and summed in bfloat16 or wider, within the bound.
No kernel may reach another device: no remote copies, remote signals or barrier semaphores. Data moves between devices by JAX's collectives and lax.ppermute only.
A program may use at most 192 MiB of HBM per device.

v0:
```python
import functools

import jax
import jax.numpy as jnp
from jax import lax
from jax.experimental import pallas as pl
from jax.experimental.pallas import tpu as pltpu
from jax.sharding import PartitionSpec as P

F32 = jnp.float32
BF16 = jnp.bfloat16
BANDS = 4
SECTORS = 32
EDGE_ROWS = 10


def mesh_pairs(partner):
    return [
        (b * SECTORS + s, (lambda t: t[0] * SECTORS + t[1] % SECTORS)(partner(b, s)))
        for b in range(BANDS)
        for s in range(SECTORS)
    ]


LON_EVEN = mesh_pairs(lambda b, s: (b, s ^ 1))
LON_ODD = mesh_pairs(lambda b, s: (b, s + 1 if s % 2 else s - 1))
LAT_OUTER = mesh_pairs(
    lambda b, s: {0: (0, s + 16), 1: (2, s), 2: (1, s), 3: (3, s + 16)}[b]
)
LAT_INNER = mesh_pairs(lambda b, s: (b ^ 1, s))


def exchange(block, pairs):
    return lax.ppermute(block, ("lat", "lon"), pairs)


def nt_dot(a, b):
    return lax.dot_general(a, b, (((1,), (1,)), ((), ())), preferred_element_type=F32)


def group_ones(size, width):
    rows = lax.broadcasted_iota(jnp.int32, (size, size), 0) // width
    cols = lax.broadcasted_iota(jnp.int32, (size, size), 1) // width
    return (rows == cols).astype(F32).astype(BF16)


def norm_gelu(v, gain, ones, width):
    sq = v * v
    hi = sq.astype(BF16)
    lo = (sq - hi.astype(F32)).astype(BF16)
    total = jnp.dot(hi, ones, preferred_element_type=F32)
    total = total + jnp.dot(lo, ones, preferred_element_type=F32)
    x = v * lax.rsqrt(total * (1.0 / width) + 1e-05) * gain
    return jax.nn.gelu(x, approximate=True)


STEP = 64
UNROLL = 16


def sums_kernel(
    target, count, btarget, bs_ref, bw_ref, s_ref, w_ref, acc_ref, m0_ref, m1_ref, bacc
):
    i = pl.program_id(0)
    odd = lax.axis_index("lon") % 2

    @pl.when(i == 0)
    def _():
        bacc[...] = jnp.zeros_like(bacc)

    def products(sr, wr, n0):
        return [
            jnp.dot(sr[n0 + u], wr[n0 + u], preferred_element_type=F32) for u in range(UNROLL)
        ]

    @pl.when(i < 2)
    def _():
        def body(j, c):
            vals = products(bs_ref, bw_ref, j * UNROLL)
            for u in range(UNROLL):
                t = btarget[i * STEP + j * UNROLL + u]
                bacc[t] += vals[u]
            return c

        lax.fori_loop(0, STEP // UNROLL, body, 0)

    @pl.when((i >= 2) & (i < 6))
    def _():
        def body(j, c):
            vals = products(s_ref, w_ref, j * UNROLL)
            for u in range(UNROLL):
                t = target[(i - 2) * STEP + j * UNROLL + u]
                acc_ref[t] = vals[u]
            return c

        lax.fori_loop(0, STEP // UNROLL, body, 0)

    @pl.when(i >= 6)
    def _():
        def body(j, c):
            vals = products(s_ref, w_ref, j * UNROLL)
            for u in range(UNROLL):
                n = (i - 2) * STEP + j * UNROLL + u
                t = jnp.where(n < count[0], target[n], 256)
                acc_ref[t] += vals[u]
            return c

        lax.fori_loop(0, STEP // UNROLL, body, 0)

    @pl.when(i == pl.num_programs(0) - 1)
    def _():
        def fill(east_ref, west_ref):
            east_ref[0:32] = bacc[32:64].astype(BF16)
            west_ref[0:32] = bacc[0:32].astype(BF16)
            for q in range(32):
                east_ref[32 + q] = acc_ref[8 * q + 7].astype(BF16)
                west_ref[32 + q] = acc_ref[8 * q].astype(BF16)

        @pl.when(odd == 0)
        def _():
            fill(m0_ref, m1_ref)

        @pl.when(odd == 1)
        def _():
            fill(m1_ref, m0_ref)


def block_sums(target, count, btarget, bstate, bweight, state, weight):
    smem = pl.BlockSpec(memory_space=pltpu.SMEM)
    border = lambda i: (jnp.minimum(i, 1), 0, 0)
    inner = lambda i: (jnp.maximum(i - 2, 0), 0, 0)
    whole = lambda i: (0, 0, 0)
    return pl.pallas_call(
        sums_kernel,
        name="block_sums",
        grid=(10,),
        in_specs=[
            smem,
            smem,
            smem,
            pl.BlockSpec((STEP, 32, 64), border),
            pl.BlockSpec((STEP, 64, 128), border),
            pl.BlockSpec((STEP, 32, 64), inner),
            pl.BlockSpec((STEP, 64, 128), inner),
        ],
        out_specs=[
            pl.BlockSpec((257, 32, 128), whole),
            pl.BlockSpec((64, 32, 128), whole),
            pl.BlockSpec((64, 32, 128), whole),
        ],
        out_shape=[
            jax.ShapeDtypeStruct((257, 32, 128), F32),
            jax.ShapeDtypeStruct((64, 32, 128), BF16),
            jax.ShapeDtypeStruct((64, 32, 128), BF16),
        ],
        scratch_shapes=[pltpu.VMEM((64, 32, 128), F32)],
        compiler_params=pltpu.CompilerParams(vmem_limit_bytes=28 << 20),
    )(target, count, btarget, bstate, bweight, state, weight)


def weights_kernel(k1_ref, k2_ref, w1_ref, w2_ref):
    w1_ref[...] = jnp.zeros_like(w1_ref)
    w2_ref[...] = jnp.zeros_like(w2_ref)
    for r in range(7):
        for s in range(7):
            for t in range(4):
                row = r * 512 + (2 * t + s + 1) * 32
                w1_ref[row : row + 32, t * 64 : (t + 1) * 64] = k1_ref[r * 7 + s]
            for t in range(2):
                row = r * 640 + (2 * t + s + 1) * 64
                w2_ref[row : row + 64, t * 128 : (t + 1) * 128] = k2_ref[r * 7 + s]


def matrix_weights(k1, k2):
    return pl.pallas_call(
        weights_kernel,
        name="matrix_weights",
        out_shape=[
            jax.ShapeDtypeStruct((3584, 256), BF16),
            jax.ShapeDtypeStruct((4480, 256), BF16),
        ],
        cost_estimate=pl.CostEstimate(flops=0, bytes_accessed=8 << 20, transcendentals=0),
        compiler_params=pltpu.CompilerParams(vmem_limit_bytes=16 << 20),
    )(k1.reshape(49, 32, 64), k2.reshape(49, 64, 128))


def field_kernel(
    acc_ref, r0_ref, r1_ref, m0_ref, m1_ref, f_ref, e_ref, ma_ref, mb_ref, fs, es, et
):
    i = pl.program_id(0)
    last = pl.num_programs(0) - 1
    odd = lax.axis_index("lon") % 2
    upper = lax.axis_index("lat") % 2
    rows = lax.broadcasted_iota(jnp.int32, (32, 128), 0)
    pix = lax.broadcasted_iota(jnp.int32, (32, 128), 1)
    pick = (pix // 4 == (rows % 8) * 4 + rows // 8).astype(F32).astype(BF16)
    keep = (
        lax.broadcasted_iota(jnp.int32, (128, 128), 0) // 32
        == lax.broadcasted_iota(jnp.int32, (128, 128), 1) % 4
    ).astype(F32).astype(BF16)

    is_odd = odd == 1
    for y in range(4):
        east_border = jnp.where(is_odd, r1_ref[0, y], r0_ref[0, y]).astype(F32)
        east_inner = jnp.where(is_odd, r1_ref[1, y], r0_ref[1, y]).astype(F32)
        west_border = jnp.where(is_odd, r0_ref[0, y], r1_ref[0, y]).astype(F32)
        west_inner = jnp.where(is_odd, r0_ref[1, y], r1_ref[1, y]).astype(F32)
        own_east = jnp.where(is_odd, m1_ref[0, y], m0_ref[0, y]).astype(F32)
        own_west = jnp.where(is_odd, m0_ref[0, y], m1_ref[0, y]).astype(F32)
        patches = [acc_ref[y * 8 + c] for c in range(8)]
        patches[0] = patches[0] + west_border
        patches[7] = patches[7] + east_border
        patches = [west_inner + own_west] + patches + [east_inner + own_east]
        for c in range(0, 10, 2):
            pair = [patches[c].astype(BF16), patches[c + 1].astype(BF16)]
            spread = jnp.concatenate(
                [jnp.concatenate([v] * 4, axis=0) * keep for v in pair], axis=0
            )
            both = nt_dot(pick, spread)
            for h in range(2):
                pc = c + h - 1
                for k in range(4):
                    v = both[8 * k : 8 * k + 8, 128 * h : 128 * h + 128]
                    g = 2 * pc + k // 2
                    kk = 4 * pc + k
                    if 0 <= pc < 8:
                        fs[y, k % 2, pl.ds(g, 8, stride=16), :] = v
                    if k % 2 == 0 and 1 <= g <= 16:
                        fs[y, 3, pl.ds(g - 1, 8, stride=16), :] = v
                    if k % 2 == 1 and -1 <= g <= 14:
                        fs[y, 2, pl.ds(g + 1, 8, stride=16), :] = v
                    if kk in (-3, -2, -1, 0, 31, 32, 33):
                        slot = kk + 3 if kk <= 0 else kk - 27
                        e_ref[slot, pl.ds(8 + 32 * i + 8 * y, 8), :] = v
                        et[y, pl.ds(slot, 8, stride=16), :] = v
        for a in range(4):
            f_ref[a, 4 * y : 4 * y + 4] = fs[y, a].astype(BF16).reshape(4, 2, 16, 128)

    @pl.when(i == 0)
    def _():
        for y in range(4):
            et[y, pl.ds(7, 8, stride=16), :] = jnp.zeros((8, 128), F32)
            for z in range(8, 16):
                et[y, pl.ds(z, 8, stride=16), :] = jnp.zeros((8, 128), F32)

    def send(ref, first):
        for a in range(4):
            ref[a] = f_ref[a, first : first + 5]
        for q in range(5):
            y, o = (first + q) // 4, (first + q) % 4
            ref[4, q] = et[y, 32 * o : 32 * o + 32].astype(BF16).reshape(2, 16, 128)

    @pl.when((i == 0) & (upper == 0))
    def _():
        send(ma_ref, 0)

    @pl.when((i == 0) & (upper == 1))
    def _():
        send(mb_ref, 0)

    @pl.when((i == last) & (upper == 0))
    def _():
        send(mb_ref, 11)

    @pl.when((i == last) & (upper == 1))
    def _():
        send(ma_ref, 11)


def build_field(acc, r0, r1, m0, m1):
    four = lambda x: x.reshape(2, 32, 32, 128)
    recv = pl.BlockSpec((2, 4, 32, 128), lambda i: (0, i, 0, 0))
    own = pl.BlockSpec((1, 4, 32, 128), lambda i: (0, i, 0, 0))
    msg = pl.BlockSpec((5, 5, 2, 16, 128), lambda i: (0, 0, 0, 0, 0))
    return pl.pallas_call(
        field_kernel,
        name="build_field",
        grid=(8,),
        in_specs=[pl.BlockSpec((32, 32, 128), lambda i: (i, 0, 0)), recv, recv, own, own],
        out_specs=[
            pl.BlockSpec((4, 16, 2, 16, 128), lambda i: (0, i, 0, 0, 0)),
            pl.BlockSpec((7, 272, 128), lambda i: (0, 0, 0)),
            msg,
            msg,
        ],
        out_shape=[
            jax.ShapeDtypeStruct((4, 128, 2, 16, 128), BF16),
            jax.ShapeDtypeStruct((7, 272, 128), F32),
            jax.ShapeDtypeStruct((5, 5, 2, 16, 128), BF16),
            jax.ShapeDtypeStruct((5, 5, 2, 16, 128), BF16),
        ],
        scratch_shapes=[
            pltpu.VMEM((4, 4, 128, 128), F32),
            pltpu.VMEM((8, 128), F32),
            pltpu.VMEM((4, 128, 128), F32),
        ],
        compiler_params=pltpu.CompilerParams(vmem_limit_bytes=20 << 20),
    )(acc, four(r0), four(r1), four(m0), four(m1))


ORDER = (2, 0, 1, 3)


def first_kernel(f_hbm, e_ref, w_ref, b_ref, g_ref, h_ref, fs, hs, ms, el, ones, sem):
    i = pl.program_id(0)

    def chunk(c):
        return pltpu.make_async_copy(
            f_hbm.at[:, pl.ds(16 * c, 16)], fs.at[:, pl.ds(2 + 16 * c, 16)], sem.at[c]
        )

    def activate(lhs):
        v = jnp.dot(lhs, w_ref[...], preferred_element_type=F32) + b_ref[...]
        return norm_gelu(v, g_ref[...], ones[...], 64)

    @pl.when(i == 0)
    def _():
        for c in range(8):
            chunk(c).start()
        ones[...] = group_ones(256, 64)
        fs[:, 0:2] = jnp.zeros((4, 2, 2, 16, 128), BF16)
        fs[:, 130:132] = jnp.zeros((4, 2, 2, 16, 128), BF16)
        for side in range(2):
            parts = []
            for r in range(7):
                for j in range(4):
                    slot = 4 * side + j
                    if slot == 7:
                        parts.append(jnp.zeros((128, 128), BF16))
                    else:
                        parts.append(e_ref[slot, pl.ds(8 - 3 + r, 128, stride=2), :].astype(BF16))
            el[side] = activate(jnp.concatenate(parts, axis=1))
        chunk(0).wait()

    @pl.when(i < 7)
    def _():
        chunk(jnp.minimum(i + 1, 7)).wait()

    parts = []
    for r in range(7):
        for a in ORDER:
            x = fs[a, pl.ds(16 * i + (r + 1) // 2, 16), (r + 1) % 2]
            parts.append(x.reshape(256, 128))
    h = activate(jnp.concatenate(parts, axis=1))
    for c in range(2):
        hs[c, 8:264] = h[:, 128 * c : 128 * c + 128]
    ms[0] = hs[0, 7:263]
    ms[1] = hs[1, 7:263]
    ms[2] = hs[0, 9:265]
    rows = pl.ds(pl.multiple_of(16 * i, 16), 16)
    ms[0, pl.ds(0, 16, stride=16), :] = el[0, rows, 0:128]
    ms[1, pl.ds(0, 16, stride=16), :] = el[0, rows, 128:256]
    ms[2, pl.ds(15, 16, stride=16), :] = el[1, rows, 0:128]
    tile = lambda v: v.astype(BF16).reshape(8, 2, 16, 128)
    h_ref[0] = tile(ms[0])
    h_ref[1] = tile(ms[1])
    h_ref[2] = tile(hs[0, 8:264])
    h_ref[3] = tile(hs[1, 8:264])
    h_ref[4] = tile(ms[2])


def first_conv(f, e, w1, bias, gain):
    const2 = lambda i: (0, 0)
    return pl.pallas_call(
        first_kernel,
        name="first_conv",
        grid=(8,),
        in_specs=[
            pl.BlockSpec(memory_space=pl.ANY),
            pl.BlockSpec((7, 272, 128), lambda i: (0, 0, 0)),
            pl.BlockSpec((3584, 256), const2),
            pl.BlockSpec((1, 256), const2),
            pl.BlockSpec((1, 256), const2),
        ],
        out_specs=pl.BlockSpec((5, 8, 2, 16, 128), lambda i: (0, i, 0, 0, 0)),
        out_shape=jax.ShapeDtypeStruct((5, 64, 2, 16, 128), BF16),
        scratch_shapes=[
            pltpu.VMEM((4, 132, 2, 16, 128), BF16),
            pltpu.VMEM((2, 272, 128), F32),
            pltpu.VMEM((3, 256, 128), F32),
            pltpu.VMEM((2, 128, 256), F32),
            pltpu.VMEM((256, 256), BF16),
            pltpu.SemaphoreType.DMA((8,)),
        ],
        cost_estimate=pl.CostEstimate(
            flops=2 * 2304 * 3584 * 256, bytes_accessed=12 << 20, transcendentals=1 << 20
        ),
        compiler_params=pltpu.CompilerParams(vmem_limit_bytes=28 << 20),
    )(f, e, w1, bias, gain)


BASES = (0, 2, 4, 11, 13, 20, 27, 29)


def second_kernel(
    h_hbm, ma_ref, mb_ref, ra_ref, rb_ref, w1_ref, w2_hbm, b1_ref, g1_ref, b2_ref, g2_ref,
    o_ref, hs, w2, ve, vf, le, ts, ms, os, ones1, ones2, sem,
):
    i = pl.program_id(0)
    lat = lax.axis_index("lat")
    odd = lat % 2 == 1
    north = lat == 0
    south = lat == 3

    @pl.when(i == 0)
    def _():
        body = pltpu.make_async_copy(h_hbm, hs.at[:, 2:66], sem.at[0])
        body.start()
        weights = pltpu.make_async_copy(w2_hbm, w2, sem.at[1])
        weights.start()
        ones1[...] = group_ones(256, 64)
        ones2[...] = group_ones(256, 128)

        def row(ref, a, m):
            return ref[a, m // 2, m % 2]

        def own_top(a, m):
            return jnp.where(odd, row(mb_ref, a, m), row(ma_ref, a, m))

        def own_bot(a, m):
            return jnp.where(odd, row(ma_ref, a, m), row(mb_ref, a, m))

        def halo_top(a, m):
            return jnp.where(odd, row(rb_ref, a, m), row(ra_ref, a, m))

        def halo_bot(a, m):
            return jnp.where(odd, row(ra_ref, a, m), row(rb_ref, a, m))

        for a in range(5):
            def put(n, v):
                if a < 4:
                    vf[a, n] = v
                else:
                    ve[16 * n : 16 * n + 16] = v.astype(F32)

            for q in range(11):
                normal = halo_top(a, q + 1) if q < 9 else own_top(a, q - 9)
                polar = own_top(a, 2 - q) if q < 3 else halo_top(a, q - 3)
                put(q, jnp.where(north, polar, normal))
            for q in range(9):
                if q < 3:
                    v = jnp.where(north, halo_top(a, 2 - q), halo_top(a, 7 + q))
                else:
                    v = own_top(a, q - 3)
                put(11 + q, v)
            for q in range(7):
                if q < 5:
                    v = own_bot(a, 5 + q)
                else:
                    v = jnp.where(south, halo_bot(a, 14 - q), halo_bot(a, q - 5))
                put(20 + q, v)
            for q in range(9):
                normal = own_bot(a, 7 + q) if q < 3 else halo_bot(a, q - 3)
                polar = halo_bot(a, 3 + q) if q < 7 else own_bot(a, 16 - q)
                put(27 + q, jnp.where(south, polar, normal))

        for n, base in enumerate(BASES):
            for r in range(7):
                for j in range(4):
                    col = 128 * (4 * r + j)
                    for side in range(2):
                        src = 16 * (base + r) + 4 * side + j
                        le[n + 8 * side : n + 8 * side + 1, col : col + 128] = ve[src : src + 1, :]
        parts = []
        for r in range(7):
            for a in ORDER:
                parts.append(jnp.concatenate([vf[a, base + r] for base in BASES], axis=0))
        lhs = jnp.concatenate([jnp.concatenate(parts, axis=1), le[...].astype(BF16)], axis=0)
        v = jnp.dot(lhs, w1_ref[...], preferred_element_type=F32) + b1_ref[...]
        h = norm_gelu(v, g1_ref[...], ones1[...], 64)
        for c in range(2):
            ts[c, 8:136] = h[0:128, 128 * c : 128 * c + 128]
        ms[0] = ts[0, 7:135]
        ms[1] = ts[1, 7:135]
        ms[2] = ts[0, 9:137]
        ms[0, pl.ds(0, 8, stride=16), :] = h[128:136, 0:128]
        ms[1, pl.ds(0, 8, stride=16), :] = h[128:136, 128:256]
        ms[2, pl.ds(15, 8, stride=16), :] = h[136:144, 0:128]
        body.wait()
        full = [ms[0], ms[1], ts[0, 8:136], ts[1, 8:136], ms[2]]
        for a in range(5):
            v = full[a].astype(BF16).reshape(8, 16, 128)
            for n in range(3):
                to = jnp.where(north, 3 - n, 1 + n)
                hs[a, to // 2, to % 2] = v[n]
            hs[a, 2, 0] = v[3]
            hs[a, 2, 1] = v[4]
            hs[a, 65, 1] = v[5]
            for n in range(2):
                to = jnp.where(south, 1 - n, n)
                hs[a, 66, to] = v[6 + n]
        weights.wait()

    parts = []
    for r in range(7):
        for a in range(5):
            x = hs[a, pl.ds(16 * i + (r + 1) // 2, 16), (r + 1) % 2]
            parts.append(x.reshape(256, 128))
    v = jnp.dot(jnp.concatenate(parts, axis=1), w2[...], preferred_element_type=F32) + b2_ref[...]
    y = norm_gelu(v, g2_ref[...], ones2[...], 128)
    for t in range(2):
        os[pl.ds(t, 256, stride=2), :] = y[:, 128 * t : 128 * t + 128]
    o_ref[...] = os[...].astype(BF16).reshape(16, 32, 128)


def second_conv(h, ma, mb, ra, rb, w1, w2, b1, g1, b2, g2):
    const2 = lambda i: (0, 0)
    msg = pl.BlockSpec((5, 5, 2, 16, 128), lambda i: (0, 0, 0, 0, 0))
    vec = pl.BlockSpec((1, 256), const2)
    return pl.pallas_call(
        second_kernel,
        name="second_conv",
        grid=(4,),
        in_specs=[
            pl.BlockSpec(memory_space=pl.ANY),
            msg,
            msg,
            msg,
            msg,
            pl.BlockSpec((3584, 256), const2),
            pl.BlockSpec(memory_space=pl.ANY),
            vec,
            vec,
            vec,
            vec,
        ],
        out_specs=pl.BlockSpec((16, 32, 128), lambda i: (i, 0, 0)),
        out_shape=jax.ShapeDtypeStruct((64, 32, 128), BF16),
        scratch_shapes=[
            pltpu.VMEM((5, 68, 2, 16, 128), BF16),
            pltpu.VMEM((4480, 256), BF16),
            pltpu.VMEM((36 * 16, 128), F32),
            pltpu.VMEM((4, 36, 16, 128), BF16),
            pltpu.VMEM((16, 3584), F32),
            pltpu.VMEM((2, 144, 128), F32),
            pltpu.VMEM((3, 128, 128), F32),
            pltpu.VMEM((512, 128), F32),
            pltpu.VMEM((256, 256), BF16),
            pltpu.VMEM((256, 256), BF16),
            pltpu.SemaphoreType.DMA((2,)),
        ],
        compiler_params=pltpu.CompilerParams(vmem_limit_bytes=28 << 20),
    )(h, ma, mb, ra, rb, w1, w2, b1, g1, b2, g2)


def local(
    cell_state,
    remap_weight,
    block_target,
    block_count,
    border_state,
    border_weight,
    border_target,
    kernel_one,
    bias_one,
    gain_one,
    kernel_two,
    bias_two,
    gain_two,
):
    acc, m0, m1 = block_sums(
        block_target[0, 0],
        block_count[0],
        border_target[0, 0],
        border_state[0, 0],
        border_weight[0, 0],
        cell_state[0, 0],
        remap_weight[0, 0],
    )
    r0 = exchange(m0, LON_EVEN)
    r1 = exchange(m1, LON_ODD)
    w1, w2 = matrix_weights(kernel_one, kernel_two)
    f, e, ma, mb = build_field(acc, r0, r1, m0, m1)
    ra = exchange(ma, LAT_OUTER)
    rb = exchange(mb, LAT_INNER)
    b1 = jnp.tile(bias_one, 4)[None]
    g1 = jnp.tile(gain_one, 4)[None]
    b2 = jnp.tile(bias_two, 2)[None]
    g2 = jnp.tile(gain_two, 2)[None]
    h = first_conv(f, e, w1, b1, g1)
    return second_conv(h, ma, mb, ra, rb, w1, w2, b1, g1, b2, g2)


def solution(mesh):
    placed = (
        P("lat", "lon", None, None, None),
        P("lat", "lon", None, None, None),
        P("lat", "lon", None),
        P("lat", "lon"),
        P("lat", "lon", None, None, None),
        P("lat", "lon", None, None, None),
        P("lat", "lon", None),
        P(),
        P(),
        P(),
        P(),
        P(),
        P(),
    )
    return jax.shard_map(
        local, mesh=mesh, in_specs=placed, out_specs=P("lat", "lon", None), check_vma=False
    )
```

profile of v0, /device:TPU:1, one launch (start us, length us, event | category | flops | bytes accessed | tf_op | source)
XLA Modules:
  0.0 79.0 jit_solution(18308042489942605610)
XLA Ops:
  0.0 0.0 copy-start.7
  0.0 0.0 copy-start.8
  0.0 0.0 copy-start.4
  0.0 7.6 %copy.15 = bf16[1,1,512,32,64]{4,3,2,1,0:T(8,128)(2,1)} copy(bf16[1,1,512,32,64]{2,4,3,1,0:T(8,128)(2,1)} %param.13) | data formatting | bytes 4194304 | tf_op args[0]
  7.6 2.5 %copy.14 = bf16[1,1,128,32,64]{4,3,2,1,0:T(8,128)(2,1)S(1)} copy(bf16[1,1,128,32,64]{2,4,3,1,0:T(8,128)(2,1)} %param.17) | data formatting | bytes 1048576 | tf_op args[4]
  10.7 0.0 copy-done.7
  10.7 0.0 copy-done.8
  10.7 0.0 copy-done.4
  10.7 0.0 copy-start
  10.7 2.2 %copy-done = bf16[1,1,512,32,64]{4,3,2,1,0:T(8,128)(2,1)S(1)} copy-done((bf16[1,1,512,32,64]{4,3,2,1,0:T(8,128)(2,1)S(1)}, bf16[1,1,512,32,64]{4,3,2,1,0:T(8,128)(2,1)}, u32[]{:S(2)}) %copy-start) | copy-done | bytes 2097176
  12.9 0.0 copy-start.1
  12.9 3.4 %copy-done.1 = bf16[1,1,512,64,128]{4,3,2,1,0:T(8,128)(2,1)S(1)} copy-done((bf16[1,1,512,64,128]{4,3,2,1,0:T(8,128)(2,1)S(1)}, bf16[1,1,512,64,128]{4,3,2,1,0:T(8,128)(2,1)}, u32[]{:S(2)}) %copy-start.1) | copy-done | bytes 8388632
  16.3 0.0 copy-start.9
  16.3 0.0 copy-start.6
  16.3 10.5 %block_sums.1 = (f32[257,32,128]{2,1,0:T(8,128)S(1)}, bf16[64,32,128]{2,1,0:T(8,128)(2,1)}, bf16[64,32,128]{2,1,0:T(8,128)(2,1)}) custom-call(s32[512]{0:T(512)S(1)} %bitcast.24, s32[1]{0:T(128)} %bitcast.15.count, s32[128]{0:T(128)S(1)} %bitcast.27, bf16[128,32,64]{2,1,0:T(8,128)(2,1)S(1)} %bitcast.18, bf16[128,64,128]{2,1,0:T(8,128)(2,1)S(1)} %bitcast.19, ...), custom_call_target="tpu_custom_call" | custom-call | tf_op jit(solution)/shard_map/block_sums/pallas_call | solution.py:133
  26.8 0.0 copy-start.2
  26.8 2.0 %copy-done.2 = f32[257,32,128]{2,1,0:T(8,128)} copy-done((f32[257,32,128]{2,1,0:T(8,128)}, f32[257,32,128]{2,1,0:T(8,128)S(1)}, u32[]{:S(2)}) %copy-start.2) | copy-done | bytes 4210712
  28.7 2.3 %collective-permute-start = (bf16[64,32,128]{2,1,0:T(8,128)(2,1)}, bf16[64,32,128]{2,1,0:T(8,128)(2,1)S(1)}, u32[]{:S(2)}, u32[]{:S(2)}) collective-permute-start(bf16[64,32,128]{2,1,0:T(8,128)(2,1)} %get-tuple-element.15), channel_id=1, source_target_pairs={{0,1},{1,0},{2,3},{3,2},{4,5},{5,4},{6,7},{7,6},{8,9},{9,8},{10,11... | collective-permute-start | bytes 1572872 | tf_op jit(solution)/shard_map/ppermute | solution.py:34
  31.1 7.0 %collective-permute-start.1 = (bf16[64,32,128]{2,1,0:T(8,128)(2,1)}, bf16[64,32,128]{2,1,0:T(8,128)(2,1)S(1)}, u32[]{:S(2)}, u32[]{:S(2)}) collective-permute-start(bf16[64,32,128]{2,1,0:T(8,128)(2,1)} %get-tuple-element.16), channel_id=1, source_target_pairs={{0,31},{1,2},{2,1},{3,4},{4,3},{5,6},{6,5},{7,8},{8,7},{9,10},{10,... | collective-permute-start | bytes 1572872 | tf_op jit(solution)/shard_map/ppermute | solution.py:34
  38.1 0.0 copy-done.9
  38.1 0.1 broadcast_in_dim_tile.12.b_ref.b1_ref
  38.1 0.7 tile.9
  38.8 0.1 broadcast_in_dim_tile.13.g_ref.g1_ref
  38.9 0.0 copy-done.6
  38.9 0.0 copy-start.5
  38.9 1.1 %copy-done.5 = bf16[7,7,64,128]{3,2,1,0:T(8,128)(2,1)S(1)} copy-done((bf16[7,7,64,128]{3,2,1,0:T(8,128)(2,1)S(1)}, bf16[7,7,64,128]{3,2,1,0:T(8,128)(2,1)}, u32[]{:S(2)}) %copy-start.5) | copy-done | bytes 802840
  40.0 0.8 %matrix_weights.1 = (bf16[3584,256]{1,0:T(8,128)(2,1)S(1)}, bf16[4480,256]{1,0:T(8,128)(2,1)S(1)}) custom-call(bf16[49,32,64]{2,1,0:T(8,128)(2,1)S(1)} %bitcast.23, bf16[49,64,128]{2,1,0:T(8,128)(2,1)S(1)} %bitcast.20), custom_call_target="tpu_custom_call" | custom-call | bytes 8388608 | tf_op jit(solution)/shard_map/matrix_weights/pallas_call | solution.py:175
  40.9 1.8 %collective-permute-done = bf16[64,32,128]{2,1,0:T(8,128)(2,1)S(1)} collective-permute-done((bf16[64,32,128]{2,1,0:T(8,128)(2,1)}, bf16[64,32,128]{2,1,0:T(8,128)(2,1)S(1)}, u32[]{:S(2)}, u32[]{:S(2)}) %collective-permute-start) | collective-permute-done | bytes 524320 | tf_op jit(solution)/shard_map/ppermute | solution.py:34
  42.7 6.9 %collective-permute-done.1 = bf16[64,32,128]{2,1,0:T(8,128)(2,1)S(1)} collective-permute-done((bf16[64,32,128]{2,1,0:T(8,128)(2,1)}, bf16[64,32,128]{2,1,0:T(8,128)(2,1)S(1)}, u32[]{:S(2)}, u32[]{:S(2)}) %collective-permute-start.1) | collective-permute-done | bytes 524320 | tf_op jit(solution)/shard_map/ppermute | solution.py:34
  49.6 0.0 copy-start.3
  49.6 2.2 %copy-done.3 = f32[257,32,128]{2,1,0:T(8,128)S(1)} copy-done((f32[257,32,128]{2,1,0:T(8,128)S(1)}, f32[257,32,128]{2,1,0:T(8,128)}, u32[]{:S(2)}) %copy-start.3) | copy-done | bytes 4210712
  51.7 6.4 %build_field.1 = (bf16[4,128,2,16,128]{4,3,2,1,0:T(8,128)(2,1)S(1)}, f32[7,272,128]{2,1,0:T(8,128)S(1)}, bf16[5,5,2,16,128]{4,3,2,1,0:T(8,128)(2,1)S(1)}, bf16[5,5,2,16,128]{4,3,2,1,0:T(8,128)(2,1)S(1)}) custom-call(f32[257,32,128]{2,1,0:T(8,128)S(1)} %copy-done.3, bf16[2,32,32,128]{3,2,1,0:T(8,128)(2,1)S(1)} %bitcast.21, ...), custom_call_target="tpu_custom_call" | custom-call | tf_op jit(solution)/shard_map/build_field/pallas_call | solution.py:275
  58.1 3.4 %collective-permute-start.2 = (bf16[5,5,2,16,128]{4,3,2,1,0:T(8,128)(2,1)S(1)}, bf16[5,5,2,16,128]{4,3,2,1,0:T(8,128)(2,1)S(1)}, u32[]{:S(2)}, u32[]{:S(2)}) collective-permute-start(bf16[5,5,2,16,128]{4,3,2,1,0:T(8,128)(2,1)S(1)} %get-tuple-element.20.ma_ref), channel_id=1, source_target_pairs={{0,16},{1,17},{2,18},{3,19},{4,20},{5,21},{6,22},{7,23},{8,24},{9,... | collective-permute-start | bytes 614408 | tf_op jit(solution)/shard_map/ppermute | solution.py:34
  61.5 0.1 collective-permute-start.3
  61.6 0.0 copy-start.10
  61.6 0.0 copy-start.11
  61.6 10.3 %first_conv.1.h_hbm = bf16[5,64,2,16,128]{4,3,2,1,0:T(8,128)(2,1)S(1)} custom-call(bf16[4,128,2,16,128]{4,3,2,1,0:T(8,128)(2,1)S(1)} %get-tuple-element.17.f_hbm, f32[7,272,128]{2,1,0:T(8,128)S(1)} %get-tuple-element.18.e_ref, bf16[3584,256]{1,0:T(8,128)(2,1)S(1)} %get-tuple-element.19.w_ref.w1_ref, f32[1,256]{1,0:T(1,128)S(1)} %broadcast_in_dim_tile.12.b_ref.b1_ref, ...), custom_call_target="tpu_custom_call" | custom-call | flops 4227858432 | bytes 12582912 | tf_op jit(solution)/shard_map/first_conv/pallas_call | solution.py:364
  71.9 0.0 collective-permute-done.2.ra_ref
  71.9 0.0 collective-permute-done.3.rb_ref
  72.0 0.0 copy-done.10
  72.0 0.0 copy-done.11
  72.0 7.0 %second_conv.1 = bf16[64,32,128]{2,1,0:T(8,128)(2,1)} custom-call(bf16[5,64,2,16,128]{4,3,2,1,0:T(8,128)(2,1)S(1)} %first_conv.1.h_hbm, bf16[5,5,2,16,128]{4,3,2,1,0:T(8,128)(2,1)S(1)} %get-tuple-element.20.ma_ref, bf16[5,5,2,16,128]{4,3,2,1,0:T(8,128)(2,1)S(1)} %get-tuple-element.21.mb_ref, bf16[5,5,2,16,128]{4,3,2,1,0:T(8,128)(2,1)S(1)} %collective-permute-done.2.ra_ref, ...), custom_call_target="tpu_custom_call" | custom-call | tf_op jit(solution)/shard_map/second_conv/pallas_call | solution.py:510
  (3 shorter events, 0.0 us)
Async XLA Ops:
  0.0 10.7 %copy-start.7 = (s32[1,1,512]{2,1,0:T(1,128)S(1)}, s32[1,1,512]{2,1,0:T(1,128)}, u32[]{:S(2)}) copy-start(s32[1,1,512]{2,1,0:T(1,128)} %param.15) | copy-start | bytes 6148
  0.0 10.7 %copy-start.8 = (s32[1,1,128]{2,1,0:T(1,128)S(1)}, s32[1,1,128]{2,1,0:T(1,128)}, u32[]{:S(2)}) copy-start(s32[1,1,128]{2,1,0:T(1,128)} %param.19) | copy-start | bytes 1540
  0.0 10.7 %copy-start.4 = (bf16[1,1,128,64,128]{4,3,2,1,0:T(8,128)(2,1)S(1)}, bf16[1,1,128,64,128]{4,3,2,1,0:T(8,128)(2,1)}, u32[]{:S(2)}) copy-start(bf16[1,1,128,64,128]{4,3,2,1,0:T(8,128)(2,1)} %param.18) | copy-start | bytes 6291460
  10.7 2.2 %copy-start = (bf16[1,1,512,32,64]{4,3,2,1,0:T(8,128)(2,1)S(1)}, bf16[1,1,512,32,64]{4,3,2,1,0:T(8,128)(2,1)}, u32[]{:S(2)}) copy-start(bf16[1,1,512,32,64]{4,3,2,1,0:T(8,128)(2,1)} %copy.15) | copy-start | bytes 6291460
  12.9 3.4 %copy-start.1 = (bf16[1,1,512,64,128]{4,3,2,1,0:T(8,128)(2,1)S(1)}, bf16[1,1,512,64,128]{4,3,2,1,0:T(8,128)(2,1)}, u32[]{:S(2)}) copy-start(bf16[1,1,512,64,128]{4,3,2,1,0:T(8,128)(2,1)} %param.14) | copy-start | bytes 25165828
  16.3 21.8 %copy-start.9 = (f32[64]{0:T(128)S(1)}, f32[64]{0:T(128)}, u32[]{:S(2)}) copy-start(f32[64]{0:T(128)} %param.21) | copy-start | bytes 772
  16.3 22.6 %copy-start.6 = (bf16[7,7,32,64]{3,2,1,0:T(8,128)(2,1)S(1)}, bf16[7,7,32,64]{3,2,1,0:T(8,128)(2,1)}, u32[]{:S(2)}) copy-start(bf16[7,7,32,64]{3,2,1,0:T(8,128)(2,1)} %param.20) | copy-start | bytes 602116
  26.8 2.0 %copy-start.2 = (f32[257,32,128]{2,1,0:T(8,128)}, f32[257,32,128]{2,1,0:T(8,128)S(1)}, u32[]{:S(2)}) copy-start(f32[257,32,128]{2,1,0:T(8,128)S(1)} %get-tuple-element.14.acc_ref) | copy-start | bytes 12632068
  28.7 13.9 %collective-permute-start = (bf16[64,32,128]{2,1,0:T(8,128)(2,1)}, bf16[64,32,128]{2,1,0:T(8,128)(2,1)S(1)}, u32[]{:S(2)}, u32[]{:S(2)}) collective-permute-start(bf16[64,32,128]{2,1,0:T(8,128)(2,1)} %get-tuple-element.15), channel_id=1, source_target_pairs={{0,1},{1,0},{2,3},{3,2},{4,5},{5,4},{6,7},{7,6},{8,9},{9,8},{10,11... | collective-permute-start | bytes 1572872 | tf_op jit(solution)/shard_map/ppermute | solution.py:34
  31.1 18.5 %collective-permute-start.1 = (bf16[64,32,128]{2,1,0:T(8,128)(2,1)}, bf16[64,32,128]{2,1,0:T(8,128)(2,1)S(1)}, u32[]{:S(2)}, u32[]{:S(2)}) collective-permute-start(bf16[64,32,128]{2,1,0:T(8,128)(2,1)} %get-tuple-element.16), channel_id=1, source_target_pairs={{0,31},{1,2},{2,1},{3,4},{4,3},{5,6},{6,5},{7,8},{8,7},{9,10},{10,... | collective-permute-start | bytes 1572872 | tf_op jit(solution)/shard_map/ppermute | solution.py:34
  38.9 1.1 %copy-start.5 = (bf16[7,7,64,128]{3,2,1,0:T(8,128)(2,1)S(1)}, bf16[7,7,64,128]{3,2,1,0:T(8,128)(2,1)}, u32[]{:S(2)}) copy-start(bf16[7,7,64,128]{3,2,1,0:T(8,128)(2,1)} %param.23) | copy-start | bytes 2408452
  49.6 2.2 %copy-start.3 = (f32[257,32,128]{2,1,0:T(8,128)S(1)}, f32[257,32,128]{2,1,0:T(8,128)}, u32[]{:S(2)}) copy-start(f32[257,32,128]{2,1,0:T(8,128)} %copy-done.2) | copy-start | bytes 12632068
  58.1 13.8 %collective-permute-start.2 = (bf16[5,5,2,16,128]{4,3,2,1,0:T(8,128)(2,1)S(1)}, bf16[5,5,2,16,128]{4,3,2,1,0:T(8,128)(2,1)S(1)}, u32[]{:S(2)}, u32[]{:S(2)}) collective-permute-start(bf16[5,5,2,16,128]{4,3,2,1,0:T(8,128)(2,1)S(1)} %get-tuple-element.20.ma_ref), channel_id=1, source_target_pairs={{0,16},{1,17},{2,18},{3,19},{4,20},{5,21},{6,22},{7,23},{8,24},{9,... | collective-permute-start | bytes 614408 | tf_op jit(solution)/shard_map/ppermute | solution.py:34
  61.5 10.5 %collective-permute-start.3 = (bf16[5,5,2,16,128]{4,3,2,1,0:T(8,128)(2,1)S(1)}, bf16[5,5,2,16,128]{4,3,2,1,0:T(8,128)(2,1)S(1)}, u32[]{:S(2)}, u32[]{:S(2)}) collective-permute-start(bf16[5,5,2,16,128]{4,3,2,1,0:T(8,128)(2,1)S(1)} %get-tuple-element.21.mb_ref), channel_id=1, source_target_pairs={{0,32},{1,33},{2,34},{3,35},{4,36},{5,37},{6,38},{7,39},{8,40},{9,... | collective-permute-start | bytes 614408 | tf_op jit(solution)/shard_map/ppermute | solution.py:34
  61.6 10.4 %copy-start.10 = (f32[128]{0:T(128)S(1)}, f32[128]{0:T(128)}, u32[]{:S(2)}) copy-start(f32[128]{0:T(128)} %param.24) | copy-start | bytes 1540
  61.6 10.4 %copy-start.11 = (f32[128]{0:T(128)S(1)}, f32[128]{0:T(128)}, u32[]{:S(2)}) copy-start(f32[128]{0:T(128)} %param.25) | copy-start | bytes 1540
where the time goes:
time: 79.9 us; the launch traced here: 79 us
  Pallas kernels  35 us (44%)
  local copies, waits for them, and re-layouts  21.7 us (27%)
  starting transfers between devices  12.8 us (16%)
  waiting for transfers between devices  8.69 us (11%)
    unnamed x26, local copies, waits for them, and re-layouts  20.9 us
    ppermute x4, starting transfers between devices, exchange(): return lax.ppermute(block, ('lat', 'lon'), pairs)  12.8 us
    pallas_call x1, Pallas kernels, block_sums(): pl.pallas_call(sums_kernel, name='block_sums', grid=(10,), in_specs=[smem...  10.5 us
    pallas_call x1, Pallas kernels, first_conv(): pl.pallas_call(first_kernel, name='first_conv', grid=(8,), in_specs=[pl.B...  10.3 us
    ppermute x4, waiting for transfers between devices, exchange(): return lax.ppermute(block, ('lat', 'lon'), pairs)  8.69 us
    pallas_call x1, Pallas kernels, second_conv(): pl.pallas_call(second_kernel, name='second_conv', grid=(4,), in_specs=[pl...  6.99 us
    pallas_call x1, Pallas kernels, build_field(): pl.pallas_call(field_kernel, name='build_field', grid=(8,), in_specs=[pl....  6.36 us
  transfers between devices with their start and end apart: 4, of which 2 were waited for; matrix products, arithmetic and copies ran while one was open for 1% of the time, Pallas kernels for 14%

commit v1 on v0

--- a/solution.py
+++ b/solution.py
@@ -1,5 +1,3 @@
-import functools
-
 import jax
 import jax.numpy as jnp
 from jax import lax
@@ -11,7 +9,7 @@
 BF16 = jnp.bfloat16
 BANDS = 4
 SECTORS = 32
-EDGE_ROWS = 10
+BIG = 24 << 20
 
 
 def mesh_pairs(partner):
@@ -54,111 +52,198 @@
     return jax.nn.gelu(x, approximate=True)
 
 
-STEP = 64
-UNROLL = 16
+def unit(size):
+    rows = lax.broadcasted_iota(jnp.int32, (size, size), 0)
+    cols = lax.broadcasted_iota(jnp.int32, (size, size), 1)
+    return (rows == cols).astype(F32).astype(BF16)
+
+
+HBM = pl.BlockSpec(memory_space=pltpu.HBM)
+SMEM = pl.BlockSpec(memory_space=pltpu.SMEM)
+VMEM = pl.BlockSpec(memory_space=pltpu.VMEM)
+
+
+def in_hbm(x):
+    return pltpu.with_memory_space_constraint(x, pltpu.HBM)
+
+
+def half_lanes():
+    lanes = lax.broadcasted_iota(jnp.int32, (16, 128), 1)
+    low = (lanes < 64).astype(F32).astype(BF16)
+    high = (lanes >= 64).astype(F32).astype(BF16)
+    return low, high
+
+
+def send_sides(m0_ref, m1_ref, east, west):
+    odd = lax.axis_index("lon") % 2
+
+    def fill(east_ref, west_ref):
+        for q in range(32):
+            east_ref[q] = east(q).astype(BF16)
+            west_ref[q] = west(q).astype(BF16)
+
+    @pl.when(odd == 0)
+    def _():
+        fill(m0_ref, m1_ref)
+
+    @pl.when(odd == 1)
+    def _():
+        fill(m1_ref, m0_ref)
+
+
+def border_kernel(btarget, x_hbm, w_hbm, m0_ref, m1_ref, token, xv, wv, st, sb, acc, sem):
+    states = pltpu.make_async_copy(x_hbm, xv, sem.at[4])
+    states.start()
+    chunks = [
+        pltpu.make_async_copy(
+            w_hbm.at[pl.ds(32 * c, 32)], wv.at[pl.ds(32 * c, 32)], sem.at[c]
+        )
+        for c in range(4)
+    ]
+    for c in chunks:
+        c.start()
+    acc[...] = jnp.zeros_like(acc)
+    low, high = half_lanes()
+    eye = unit(128)
+    states.wait()
+    for c in range(0, 16, 2):
+        x = jnp.concatenate([xv[c], xv[c + 16], xv[c + 1], xv[c + 17]], axis=0)
+        out = nt_dot(eye, x)
+        st[pl.ds(c, 128, stride=16), :] = out[:, :128]
+        st[pl.ds(c + 1, 128, stride=16), :] = out[:, 128:]
+    for q in range(8):
+        sb[16 * q : 16 * q + 16] = st[256 * q : 256 * q + 256].astype(BF16).reshape(16, 16, 128)
+    for c in range(4):
+        chunks[c].wait()
+
+        def body(carry, c=c):
+            n0 = 32 * c
+            vals = []
+            for u in range(0, 32, 2):
+                rows = [sb[n0 + u + k] * half for k in range(2) for half in (low, high)]
+                w = jnp.concatenate([wv[n0 + u], wv[n0 + u + 1]], axis=1)
+                rhs = jnp.concatenate([w, w], axis=0)
+                vals.append(
+                    jnp.dot(jnp.concatenate(rows, axis=0), rhs, preferred_element_type=F32)
+                )
+            for u in range(32):
+                k = u % 2
+                acc[btarget[n0 + u]] += vals[u // 2][32 * k : 32 * k + 32, 128 * k : 128 * k + 128]
+            return carry
+
+        body(0)
+    send_sides(m0_ref, m1_ref, lambda q: acc[32 + q], lambda q: acc[q])
+    token[...] = jnp.zeros_like(token)
+
+
+def border_sums(btarget, bstate, bweight):
+    side = jax.ShapeDtypeStruct((32, 32, 128), BF16)
+    return pl.pallas_call(
+        border_kernel,
+        name="border_sums",
+        in_specs=[SMEM, HBM, HBM],
+        out_specs=[VMEM, VMEM, VMEM],
+        out_shape=[side, side, jax.ShapeDtypeStruct((8, 128), F32)],
+        scratch_shapes=[
+            pltpu.VMEM((32, 64, 128), BF16),
+            pltpu.VMEM((128, 64, 128), BF16),
+            pltpu.VMEM((2048, 128), F32),
+            pltpu.VMEM((128, 16, 128), BF16),
+            pltpu.VMEM((64, 32, 128), F32),
+            pltpu.SemaphoreType.DMA((5,)),
+        ],
+        cost_estimate=pl.CostEstimate(
+            flops=2 * 128 * 32 * 64 * 128, bytes_accessed=4 << 20, transcendentals=0
+        ),
+        compiler_params=pltpu.CompilerParams(vmem_limit_bytes=BIG),
+    )(btarget, in_hbm(jnp.transpose(bstate, (1, 2, 0))), in_hbm(bweight))
 
 
 def sums_kernel(
-    target, count, btarget, bs_ref, bw_ref, s_ref, w_ref, acc_ref, m0_ref, m1_ref, bacc
+    target, count, after, x_hbm, w_hbm, acc_ref, m0_ref, m1_ref, xv, wv, st, sb, xsem, wsem
 ):
-    i = pl.program_id(0)
-    odd = lax.axis_index("lon") % 2
-
-    @pl.when(i == 0)
-    def _():
-        bacc[...] = jnp.zeros_like(bacc)
-
-    def products(sr, wr, n0):
-        return [
-            jnp.dot(sr[n0 + u], wr[n0 + u], preferred_element_type=F32) for u in range(UNROLL)
-        ]
-
-    @pl.when(i < 2)
-    def _():
-        def body(j, c):
-            vals = products(bs_ref, bw_ref, j * UNROLL)
-            for u in range(UNROLL):
-                t = btarget[i * STEP + j * UNROLL + u]
-                bacc[t] += vals[u]
-            return c
-
-        lax.fori_loop(0, STEP // UNROLL, body, 0)
-
-    @pl.when((i >= 2) & (i < 6))
-    def _():
-        def body(j, c):
-            vals = products(s_ref, w_ref, j * UNROLL)
-            for u in range(UNROLL):
-                t = target[(i - 2) * STEP + j * UNROLL + u]
-                acc_ref[t] = vals[u]
-            return c
-
-        lax.fori_loop(0, STEP // UNROLL, body, 0)
-
-    @pl.when(i >= 6)
-    def _():
-        def body(j, c):
-            vals = products(s_ref, w_ref, j * UNROLL)
-            for u in range(UNROLL):
-                n = (i - 2) * STEP + j * UNROLL + u
-                t = jnp.where(n < count[0], target[n], 256)
-                acc_ref[t] += vals[u]
-            return c
-
-        lax.fori_loop(0, STEP // UNROLL, body, 0)
-
-    @pl.when(i == pl.num_programs(0) - 1)
-    def _():
-        def fill(east_ref, west_ref):
-            east_ref[0:32] = bacc[32:64].astype(BF16)
-            west_ref[0:32] = bacc[0:32].astype(BF16)
-            for q in range(32):
-                east_ref[32 + q] = acc_ref[8 * q + 7].astype(BF16)
-                west_ref[32 + q] = acc_ref[8 * q].astype(BF16)
-
-        @pl.when(odd == 0)
-        def _():
-            fill(m0_ref, m1_ref)
-
-        @pl.when(odd == 1)
-        def _():
-            fill(m1_ref, m0_ref)
-
-
-def block_sums(target, count, btarget, bstate, bweight, state, weight):
-    smem = pl.BlockSpec(memory_space=pltpu.SMEM)
-    border = lambda i: (jnp.minimum(i, 1), 0, 0)
-    inner = lambda i: (jnp.maximum(i - 2, 0), 0, 0)
-    whole = lambda i: (0, 0, 0)
+    states = [
+        pltpu.make_async_copy(x_hbm.at[:, :, pl.ds(256 * p, 256)], xv.at[p], xsem.at[p])
+        for p in range(2)
+    ]
+    chunks = {
+        (p, c, h): pltpu.make_async_copy(
+            w_hbm.at[pl.ds(256 * p + 128 * h + 32 * c, 32)],
+            wv.at[pl.ds(256 * p + 128 * h + 32 * c, 32)],
+            wsem.at[p, c, h],
+        )
+        for p in range(2)
+        for c in range(4)
+        for h in range(2)
+    }
+    for p in range(2):
+        states[p].start()
+        for c in range(4):
+            for h in range(2):
+                chunks[p, c, h].start()
+    low, high = half_lanes()
+    low = jnp.concatenate([low, low], axis=0)
+    high = jnp.concatenate([high, high], axis=0)
+    eye = unit(128)
+    for p in range(2):
+        states[p].wait()
+        for c in range(0, 32, 2):
+            x = jnp.concatenate(
+                [xv[p, c + k, :, 128 * h : 128 * h + 128] for k in range(2) for h in range(2)], axis=0
+            )
+            out = nt_dot(eye, x)
+            st[pl.ds(c, 128, stride=32), :] = out[:, :128]
+            st[pl.ds(c + 1, 128, stride=32), :] = out[:, 128:]
+        for q in range(16):
+            sb[8 * q : 8 * q + 8] = st[256 * q : 256 * q + 256].astype(BF16).reshape(8, 32, 128)
+        for c in range(4):
+            chunks[p, c, 0].wait()
+            chunks[p, c, 1].wait()
+
+            n0 = 32 * c
+            for u in range(0, 32, 2):
+                rows = [sb[n0 + u + k] * half for k in range(2) for half in (low, high)]
+                cols = [
+                    [wv[256 * p + 128 * h + n0 + u + k] for k in range(2)] for h in range(2)
+                ]
+                rhs = jnp.concatenate([jnp.concatenate(r, axis=1) for r in cols], axis=0)
+                both = jnp.dot(jnp.concatenate(rows, axis=0), rhs, preferred_element_type=F32)
+                for k in range(2):
+                    for h in range(2):
+                        n = 256 * p + 128 * h + n0 + u + k
+                        at = 64 * k + 32 * h
+                        v = both[at : at + 32, 128 * k : 128 * k + 128]
+                        if p == 0:
+                            acc_ref[target[n]] = v
+                        else:
+                            acc_ref[jnp.where(n < count[0], target[n], 256)] += v
+    send_sides(m0_ref, m1_ref, lambda q: acc_ref[8 * q + 7], lambda q: acc_ref[8 * q])
+
+
+def inner_sums(target, count, after, state, weight):
+    side = jax.ShapeDtypeStruct((32, 32, 128), BF16)
     return pl.pallas_call(
         sums_kernel,
-        name="block_sums",
-        grid=(10,),
-        in_specs=[
-            smem,
-            smem,
-            smem,
-            pl.BlockSpec((STEP, 32, 64), border),
-            pl.BlockSpec((STEP, 64, 128), border),
-            pl.BlockSpec((STEP, 32, 64), inner),
-            pl.BlockSpec((STEP, 64, 128), inner),
-        ],
-        out_specs=[
-            pl.BlockSpec((257, 32, 128), whole),
-            pl.BlockSpec((64, 32, 128), whole),
-            pl.BlockSpec((64, 32, 128), whole),
-        ],
-        out_shape=[
-            jax.ShapeDtypeStruct((257, 32, 128), F32),
-            jax.ShapeDtypeStruct((64, 32, 128), BF16),
-            jax.ShapeDtypeStruct((64, 32, 128), BF16),
-        ],
-        scratch_shapes=[pltpu.VMEM((64, 32, 128), F32)],
-        compiler_params=pltpu.CompilerParams(vmem_limit_bytes=28 << 20),
-    )(target, count, btarget, bstate, bweight, state, weight)
-
-
-def weights_kernel(k1_ref, k2_ref, w1_ref, w2_ref):
+        name="inner_sums",
+        in_specs=[SMEM, SMEM, VMEM, HBM, HBM],
+        out_specs=[VMEM, VMEM, VMEM],
+        out_shape=[pltpu.VMEM((257, 32, 128), F32), side, side],
+        scratch_shapes=[
+            pltpu.VMEM((2, 32, 64, 256), BF16),
+            pltpu.VMEM((512, 64, 128), BF16),
+            pltpu.VMEM((4096, 128), F32),
+            pltpu.VMEM((128, 32, 128), BF16),
+            pltpu.SemaphoreType.DMA((2,)),
+            pltpu.SemaphoreType.DMA((2, 4, 2)),
+        ],
+        cost_estimate=pl.CostEstimate(
+            flops=2 * 512 * 32 * 64 * 128, bytes_accessed=16 << 20, transcendentals=0
+        ),
+        compiler_params=pltpu.CompilerParams(vmem_limit_bytes=BIG),
+    )(target, count, after, in_hbm(jnp.transpose(state, (1, 2, 0))), in_hbm(weight))
+
+
+def weights_kernel(k1_ref, k2_ref, b1_ref, g1_ref, b2_ref, g2_ref, w1_ref, w2_ref, v_ref):
     w1_ref[...] = jnp.zeros_like(w1_ref)
     w2_ref[...] = jnp.zeros_like(w2_ref)
     for r in range(7):
@@ -169,23 +254,30 @@
             for t in range(2):
                 row = r * 640 + (2 * t + s + 1) * 64
                 w2_ref[row : row + 64, t * 128 : (t + 1) * 128] = k2_ref[r * 7 + s]
-
-
-def matrix_weights(k1, k2):
+    for t in range(4):
+        v_ref[0:1, t * 64 : (t + 1) * 64] = b1_ref[...]
+        v_ref[1:2, t * 64 : (t + 1) * 64] = g1_ref[...]
+    for t in range(2):
+        v_ref[2:3, t * 128 : (t + 1) * 128] = b2_ref[...]
+        v_ref[3:4, t * 128 : (t + 1) * 128] = g2_ref[...]
+
+
+def matrix_weights(k1, k2, b1, g1, b2, g2):
     return pl.pallas_call(
         weights_kernel,
         name="matrix_weights",
         out_shape=[
             jax.ShapeDtypeStruct((3584, 256), BF16),
             jax.ShapeDtypeStruct((4480, 256), BF16),
+            jax.ShapeDtypeStruct((8, 256), F32),
         ],
         cost_estimate=pl.CostEstimate(flops=0, bytes_accessed=8 << 20, transcendentals=0),
         compiler_params=pltpu.CompilerParams(vmem_limit_bytes=16 << 20),
-    )(k1.reshape(49, 32, 64), k2.reshape(49, 64, 128))
+    )(k1.reshape(49, 32, 64), k2.reshape(49, 64, 128), b1[None], g1[None], b2[None], g2[None])
 
 
 def field_kernel(
-    acc_ref, r0_ref, r1_ref, m0_ref, m1_ref, f_ref, e_ref, ma_ref, mb_ref, fs, es, et
+    acc, rb0_ref, rb1_ref, ri0_ref, ri1_ref, m0_ref, m1_ref, f_ref, e_ref, ma_ref, mb_ref, fs, et
 ):
     i = pl.program_id(0)
     last = pl.num_programs(0) - 1
@@ -201,13 +293,13 @@
 
     is_odd = odd == 1
     for y in range(4):
-        east_border = jnp.where(is_odd, r1_ref[0, y], r0_ref[0, y]).astype(F32)
-        east_inner = jnp.where(is_odd, r1_ref[1, y], r0_ref[1, y]).astype(F32)
-        west_border = jnp.where(is_odd, r0_ref[0, y], r1_ref[0, y]).astype(F32)
-        west_inner = jnp.where(is_odd, r0_ref[1, y], r1_ref[1, y]).astype(F32)
-        own_east = jnp.where(is_odd, m1_ref[0, y], m0_ref[0, y]).astype(F32)
-        own_west = jnp.where(is_odd, m0_ref[0, y], m1_ref[0, y]).astype(F32)
-        patches = [acc_ref[y * 8 + c] for c in range(8)]
+        east_border = jnp.where(is_odd, rb1_ref[y], rb0_ref[y]).astype(F32)
+        east_inner = jnp.where(is_odd, ri1_ref[y], ri0_ref[y]).astype(F32)
+        west_border = jnp.where(is_odd, rb0_ref[y], rb1_ref[y]).astype(F32)
+        west_inner = jnp.where(is_odd, ri0_ref[y], ri1_ref[y]).astype(F32)
+        own_east = jnp.where(is_odd, m1_ref[y], m0_ref[y]).astype(F32)
+        own_west = jnp.where(is_odd, m0_ref[y], m1_ref[y]).astype(F32)
+        patches = [acc[32 * i + 8 * y + c] for c in range(8)]
         patches[0] = patches[0] + west_border
         patches[7] = patches[7] + east_border
         patches = [west_inner + own_west] + patches + [east_inner + own_east]
@@ -267,16 +359,14 @@
         send(ma_ref, 11)
 
 
-def build_field(acc, r0, r1, m0, m1):
-    four = lambda x: x.reshape(2, 32, 32, 128)
-    recv = pl.BlockSpec((2, 4, 32, 128), lambda i: (0, i, 0, 0))
-    own = pl.BlockSpec((1, 4, 32, 128), lambda i: (0, i, 0, 0))
+def build_field(acc, *sides):
+    side = pl.BlockSpec((4, 32, 128), lambda i: (i, 0, 0))
     msg = pl.BlockSpec((5, 5, 2, 16, 128), lambda i: (0, 0, 0, 0, 0))
     return pl.pallas_call(
         field_kernel,
         name="build_field",
         grid=(8,),
-        in_specs=[pl.BlockSpec((32, 32, 128), lambda i: (i, 0, 0)), recv, recv, own, own],
+        in_specs=[VMEM] + [side] * 6,
         out_specs=[
             pl.BlockSpec((4, 16, 2, 16, 128), lambda i: (0, i, 0, 0, 0)),
             pl.BlockSpec((7, 272, 128), lambda i: (0, 0, 0)),
@@ -291,17 +381,16 @@
         ],
         scratch_shapes=[
             pltpu.VMEM((4, 4, 128, 128), F32),
-            pltpu.VMEM((8, 128), F32),
             pltpu.VMEM((4, 128, 128), F32),
         ],
-        compiler_params=pltpu.CompilerParams(vmem_limit_bytes=20 << 20),
-    )(acc, four(r0), four(r1), four(m0), four(m1))
+        compiler_params=pltpu.CompilerParams(vmem_limit_bytes=24 << 20),
+    )(acc, *sides)
 
 
 ORDER = (2, 0, 1, 3)
 
 
-def first_kernel(f_hbm, e_ref, w_ref, b_ref, g_ref, h_ref, fs, hs, ms, el, ones, sem):
+def first_kernel(f_hbm, e_ref, w_ref, v_ref, h_ref, fs, hs, ms, el, ones, sem):
     i = pl.program_id(0)
 
     def chunk(c):
@@ -310,8 +399,8 @@
         )
 
     def activate(lhs):
-        v = jnp.dot(lhs, w_ref[...], preferred_element_type=F32) + b_ref[...]
-        return norm_gelu(v, g_ref[...], ones[...], 64)
+        v = jnp.dot(lhs, w_ref[...], preferred_element_type=F32) + v_ref[0:1]
+        return norm_gelu(v, v_ref[1:2], ones[...], 64)
 
     @pl.when(i == 0)
     def _():
@@ -332,52 +421,54 @@
             el[side] = activate(jnp.concatenate(parts, axis=1))
         chunk(0).wait()
 
-    @pl.when(i < 7)
-    def _():
-        chunk(jnp.minimum(i + 1, 7)).wait()
+    for z in range(4):
+
+        @pl.when(4 * i + z < 7)
+        def _():
+            chunk(jnp.minimum(4 * i + z + 1, 7)).wait()
+
 
     parts = []
     for r in range(7):
         for a in ORDER:
-            x = fs[a, pl.ds(16 * i + (r + 1) // 2, 16), (r + 1) % 2]
-            parts.append(x.reshape(256, 128))
+            x = fs[a, pl.ds(64 * i + (r + 1) // 2, 64), (r + 1) % 2]
+            parts.append(x.reshape(1024, 128))
     h = activate(jnp.concatenate(parts, axis=1))
     for c in range(2):
-        hs[c, 8:264] = h[:, 128 * c : 128 * c + 128]
-    ms[0] = hs[0, 7:263]
-    ms[1] = hs[1, 7:263]
-    ms[2] = hs[0, 9:265]
-    rows = pl.ds(pl.multiple_of(16 * i, 16), 16)
-    ms[0, pl.ds(0, 16, stride=16), :] = el[0, rows, 0:128]
-    ms[1, pl.ds(0, 16, stride=16), :] = el[0, rows, 128:256]
-    ms[2, pl.ds(15, 16, stride=16), :] = el[1, rows, 0:128]
-    tile = lambda v: v.astype(BF16).reshape(8, 2, 16, 128)
+        hs[c, 8:1032] = h[:, 128 * c : 128 * c + 128]
+    ms[0] = hs[0, 7:1031]
+    ms[1] = hs[1, 7:1031]
+    ms[2] = hs[0, 9:1033]
+    rows = pl.ds(pl.multiple_of(64 * i, 64), 64)
+    ms[0, pl.ds(0, 64, stride=16), :] = el[0, rows, 0:128]
+    ms[1, pl.ds(0, 64, stride=16), :] = el[0, rows, 128:256]
+    ms[2, pl.ds(15, 64, stride=16), :] = el[1, rows, 0:128]
+    tile = lambda v: v.astype(BF16).reshape(32, 2, 16, 128)
     h_ref[0] = tile(ms[0])
     h_ref[1] = tile(ms[1])
-    h_ref[2] = tile(hs[0, 8:264])
-    h_ref[3] = tile(hs[1, 8:264])
+    h_ref[2] = tile(hs[0, 8:1032])
+    h_ref[3] = tile(hs[1, 8:1032])
     h_ref[4] = tile(ms[2])
 
 
-def first_conv(f, e, w1, bias, gain):
+def first_conv(f, e, w1, vec):
     const2 = lambda i: (0, 0)
     return pl.pallas_call(
         first_kernel,
         name="first_conv",
-        grid=(8,),
+        grid=(2,),
         in_specs=[
             pl.BlockSpec(memory_space=pl.ANY),
             pl.BlockSpec((7, 272, 128), lambda i: (0, 0, 0)),
             pl.BlockSpec((3584, 256), const2),
-            pl.BlockSpec((1, 256), const2),
-            pl.BlockSpec((1, 256), const2),
-        ],
-        out_specs=pl.BlockSpec((5, 8, 2, 16, 128), lambda i: (0, i, 0, 0, 0)),
+            pl.BlockSpec((8, 256), const2),
+        ],
+        out_specs=pl.BlockSpec((5, 32, 2, 16, 128), lambda i: (0, i, 0, 0, 0)),
         out_shape=jax.ShapeDtypeStruct((5, 64, 2, 16, 128), BF16),
         scratch_shapes=[
             pltpu.VMEM((4, 132, 2, 16, 128), BF16),
-            pltpu.VMEM((2, 272, 128), F32),
-            pltpu.VMEM((3, 256, 128), F32),
+            pltpu.VMEM((2, 1040, 128), F32),
+            pltpu.VMEM((3, 1024, 128), F32),
             pltpu.VMEM((2, 128, 256), F32),
             pltpu.VMEM((256, 256), BF16),
             pltpu.SemaphoreType.DMA((8,)),
@@ -386,14 +477,14 @@
             flops=2 * 2304 * 3584 * 256, bytes_accessed=12 << 20, transcendentals=1 << 20
         ),
         compiler_params=pltpu.CompilerParams(vmem_limit_bytes=28 << 20),
-    )(f, e, w1, bias, gain)
+    )(f, e, w1, vec)
 
 
 BASES = (0, 2, 4, 11, 13, 20, 27, 29)
 
 
 def second_kernel(
-    h_hbm, ma_ref, mb_ref, ra_ref, rb_ref, w1_ref, w2_hbm, b1_ref, g1_ref, b2_ref, g2_ref,
+    h_hbm, ma_ref, mb_ref, ra_ref, rb_ref, w1_ref, w2_hbm, v_ref,
     o_ref, hs, w2, ve, vf, le, ts, ms, os, ones1, ones2, sem,
 ):
     i = pl.program_id(0)
@@ -466,8 +557,8 @@
             for a in ORDER:
                 parts.append(jnp.concatenate([vf[a, base + r] for base in BASES], axis=0))
         lhs = jnp.concatenate([jnp.concatenate(parts, axis=1), le[...].astype(BF16)], axis=0)
-        v = jnp.dot(lhs, w1_ref[...], preferred_element_type=F32) + b1_ref[...]
-        h = norm_gelu(v, g1_ref[...], ones1[...], 64)
+        v = jnp.dot(lhs, w1_ref[...], preferred_element_type=F32) + v_ref[0:1]
+        h = norm_gelu(v, v_ref[1:2], ones1[...], 64)
         for c in range(2):
             ts[c, 8:136] = h[0:128, 128 * c : 128 * c + 128]
         ms[0] = ts[0, 7:135]
@@ -496,17 +587,16 @@
         for a in range(5):
             x = hs[a, pl.ds(16 * i + (r + 1) // 2, 16), (r + 1) % 2]
             parts.append(x.reshape(256, 128))
-    v = jnp.dot(jnp.concatenate(parts, axis=1), w2[...], preferred_element_type=F32) + b2_ref[...]
-    y = norm_gelu(v, g2_ref[...], ones2[...], 128)
+    v = jnp.dot(jnp.concatenate(parts, axis=1), w2[...], preferred_element_type=F32) + v_ref[2:3]
+    y = norm_gelu(v, v_ref[3:4], ones2[...], 128)
     for t in range(2):
         os[pl.ds(t, 256, stride=2), :] = y[:, 128 * t : 128 * t + 128]
     o_ref[...] = os[...].astype(BF16).reshape(16, 32, 128)
 
 
-def second_conv(h, ma, mb, ra, rb, w1, w2, b1, g1, b2, g2):
+def second_conv(h, ma, mb, ra, rb, w1, w2, vec):
     const2 = lambda i: (0, 0)
     msg = pl.BlockSpec((5, 5, 2, 16, 128), lambda i: (0, 0, 0, 0, 0))
-    vec = pl.BlockSpec((1, 256), const2)
     return pl.pallas_call(
         second_kernel,
         name="second_conv",
@@ -519,10 +609,7 @@
             msg,
             pl.BlockSpec((3584, 256), const2),
             pl.BlockSpec(memory_space=pl.ANY),
-            vec,
-            vec,
-            vec,
-            vec,
+            pl.BlockSpec((8, 256), const2),
         ],
         out_specs=pl.BlockSpec((16, 32, 128), lambda i: (i, 0, 0)),
         out_shape=jax.ShapeDtypeStruct((64, 32, 128), BF16),
@@ -540,7 +627,7 @@
             pltpu.SemaphoreType.DMA((2,)),
         ],
         compiler_params=pltpu.CompilerParams(vmem_limit_bytes=28 << 20),
-    )(h, ma, mb, ra, rb, w1, w2, b1, g1, b2, g2)
+    )(h, ma, mb, ra, rb, w1, w2, vec)
 
 
 def local(
@@ -558,27 +645,20 @@
     bias_two,
     gain_two,
 ):
-    acc, m0, m1 = block_sums(
-        block_target[0, 0],
-        block_count[0],
-        border_target[0, 0],
-        border_state[0, 0],
-        border_weight[0, 0],
-        cell_state[0, 0],
-        remap_weight[0, 0],
+    m0, m1, after = border_sums(border_target[0, 0], border_state[0, 0], border_weight[0, 0])
+    rb0 = exchange(m0, LON_EVEN)
+    rb1 = exchange(m1, LON_ODD)
+    acc, i0, i1 = inner_sums(
+        block_target[0, 0], block_count[0], after, cell_state[0, 0], remap_weight[0, 0]
     )
-    r0 = exchange(m0, LON_EVEN)
-    r1 = exchange(m1, LON_ODD)
-    w1, w2 = matrix_weights(kernel_one, kernel_two)
-    f, e, ma, mb = build_field(acc, r0, r1, m0, m1)
+    ri0 = exchange(i0, LON_EVEN)
+    ri1 = exchange(i1, LON_ODD)
+    w1, w2, vec = matrix_weights(kernel_one, kernel_two, bias_one, gain_one, bias_two, gain_two)
+    f, e, ma, mb = build_field(acc, rb0, rb1, ri0, ri1, m0, m1)
     ra = exchange(ma, LAT_OUTER)
     rb = exchange(mb, LAT_INNER)
-    b1 = jnp.tile(bias_one, 4)[None]
-    g1 = jnp.tile(gain_one, 4)[None]
-    b2 = jnp.tile(bias_two, 2)[None]
-    g2 = jnp.tile(gain_two, 2)[None]
-    h = first_conv(f, e, w1, b1, g1)
-    return second_conv(h, ma, mb, ra, rb, w1, w2, b1, g1, b2, g2)
+    h = first_conv(f, e, w1, vec)
+    return second_conv(h, ma, mb, ra, rb, w1, w2, vec)
 
 
 def solution(mesh):

time: 79.9 us -> 62 us (0.78)
  local copies, waits for them, and re-layouts: 21.7 us -> 0.69 us
  waiting for transfers between devices: 8.69 us -> 10.6 us
  Pallas kernels: 35 us -> 36.4 us
    unnamed x26 -> x16, local copies, waits for them, and re-layouts: 20.9 us -> 0.69 us
    ppermute x4 -> x6, waiting for transfers between devices: 8.69 us -> 10.6 us  [exchange(): return lax.ppermute(block, ('lat', 'lon'), pairs)]
    pallas_call x3 -> x4, Pallas kernels: 27.2 us -> 28.6 us  [the longest x1 11.6 us: inner_sums(): pl.pallas_call(sums_kernel, name='inner_sums', in_specs=[SMEM, SMEM, VMEM...]
    another operation x6 -> x0, local copies, waits for them, and re-layouts: 0.83 us -> none  [the longest x2 0.74 us: local(): g1 = jnp.tile(gain_one, 4)[None]]
    ppermute x4 -> x6, starting transfers between devices: 12.8 us -> 13.2 us  [exchange(): return lax.ppermute(block, ('lat', 'lon'), pairs)]
  transfers between devices with their start and end apart: 4 -> 6, of which waited for: 2 -> 3; matrix products, arithmetic and copies ran while one was open for 1% -> 0% of each run, Pallas kernels for 14% -> 15%
where the time goes in v1:
time: 62 us; the launch traced here: 61.8 us
  Pallas kernels  36.4 us (59%)
  starting transfers between devices  13.2 us (21%)
  waiting for transfers between devices  10.6 us (17%)
  between operations  0.98 us (2%)
  local copies, waits for them, and re-layouts  0.69 us (1%)
    ppermute x6, starting transfers between devices, exchange(): return lax.ppermute(block, ('lat', 'lon'), pairs)  13.2 us
    pallas_call x1, Pallas kernels, inner_sums(): pl.pallas_call(sums_kernel, name='inner_sums', in_specs=[SMEM, SMEM, VMEM...  11.6 us
    ppermute x6, waiting for transfers between devices, exchange(): return lax.ppermute(block, ('lat', 'lon'), pairs)  10.6 us
    pallas_call x1, Pallas kernels, first_conv(): pl.pallas_call(first_kernel, name='first_conv', grid=(2,), in_specs=[pl.B...  8.48 us
    pallas_call x1, Pallas kernels, second_conv(): pl.pallas_call(second_kernel, name='second_conv', grid=(4,), in_specs=[pl...  6.99 us
    pallas_call x1, Pallas kernels, build_field(): pl.pallas_call(field_kernel, name='build_field', grid=(8,), in_specs=[VME...  5 us
    pallas_call x1, Pallas kernels, border_sums(): pl.pallas_call(border_kernel, name='border_sums', in_specs=[SMEM, HBM, HB...  3.49 us
  transfers between devices with their start and end apart: 6, of which 3 were waited for; matrix products, arithmetic and copies ran while one was open for 0% of the time, Pallas kernels for 15%

profile of v1, /device:TPU:1, one launch (start us, length us, event | category | flops | bytes accessed | tf_op | source)
XLA Modules:
  0.0 61.8 jit_solution(14774770011792594516)
XLA Ops:
  0.0 0.0 copy-start.2
  0.7 0.0 copy-start.7
  0.7 0.6 %copy-done.7 = s32[1,1,128]{2,1,0:T(1,128)S(1)} copy-done((s32[1,1,128]{2,1,0:T(1,128)S(1)}, s32[1,1,128]{2,1,0:T(1,128)}, u32[]{:S(2)}) %copy-start.7) | copy-done | bytes 536
  1.3 3.5 %border_sums.1 = (bf16[32,32,128]{2,1,0:T(8,128)(2,1)S(1)}, bf16[32,32,128]{2,1,0:T(8,128)(2,1)S(1)}, f32[8,128]{1,0:T(8,128)S(1)}) custom-call(s32[128]{0:T(128)S(1)} %bitcast.25, bf16[32,64,128]{2,1,0:T(8,128)(2,1)} %bitcast.29, bf16[128,64,128]{2,1,0:T(8,128)(2,1)} %bitcast.27), custom_call_target="tpu_custom_call" | custom-call | flops 67108864 | bytes 4194304 | tf_op jit(solution)/shard_map/border_sums/pallas_call | solution.py:141
  4.8 0.0 copy-done.2
  4.8 0.0 copy-start
  4.8 0.0 copy-start.1
  4.9 0.0 copy-start.3
  4.9 0.0 copy-start.4
  4.9 0.0 copy-start.5
  4.9 0.0 copy-start.6
  4.9 11.6 %inner_sums.1 = (f32[257,32,128]{2,1,0:T(8,128)S(1)}, bf16[32,32,128]{2,1,0:T(8,128)(2,1)S(1)}, bf16[32,32,128]{2,1,0:T(8,128)(2,1)S(1)}) custom-call(s32[512]{0:T(512)S(1)} %bitcast.20, s32[1]{0:T(128)} %bitcast.17.count, f32[8,128]{1,0:T(8,128)S(1)} %get-tuple-element.18.after, bf16[32,64,512]{2,1,0:T(8,128)(2,1)} %bitcast.28, bf16[512,64,128]{2,1,0:T(8,128)(2,1)} %bitcast.26), custom_call_target="tpu_custom_call" | custom-call | flops 268435456 | bytes 16777216 | tf_op jit(solution)/shard_map/inner_sums/pallas_call | solution.py:225
  16.5 2.2 %collective-permute-start.2 = (bf16[32,32,128]{2,1,0:T(8,128)(2,1)S(1)}, bf16[32,32,128]{2,1,0:T(8,128)(2,1)S(1)}, u32[]{:S(2)}, u32[]{:S(2)}) collective-permute-start(bf16[32,32,128]{2,1,0:T(8,128)(2,1)S(1)} %get-tuple-element.22), channel_id=1, source_target_pairs={{0,1},{1,0},{2,3},{3,2},{4,5},{5,4},{6,7},{7,6},{8,9},{9,8},{10,11... | collective-permute-start | bytes 786440 | tf_op jit(solution)/shard_map/ppermute | solution.py:32
  18.7 7.4 %collective-permute-start.3 = (bf16[32,32,128]{2,1,0:T(8,128)(2,1)S(1)}, bf16[32,32,128]{2,1,0:T(8,128)(2,1)S(1)}, u32[]{:S(2)}, u32[]{:S(2)}) collective-permute-start(bf16[32,32,128]{2,1,0:T(8,128)(2,1)S(1)} %get-tuple-element.23), channel_id=1, source_target_pairs={{0,31},{1,2},{2,1},{3,4},{4,3},{5,6},{6,5},{7,8},{8,7},{9,10},{10,... | collective-permute-start | bytes 786440 | tf_op jit(solution)/shard_map/ppermute | solution.py:32
  26.1 0.0 collective-permute-start
  26.1 0.9 %collective-permute-start.1 = (bf16[32,32,128]{2,1,0:T(8,128)(2,1)S(1)}, bf16[32,32,128]{2,1,0:T(8,128)(2,1)S(1)}, u32[]{:S(2)}, u32[]{:S(2)}) collective-permute-start(bf16[32,32,128]{2,1,0:T(8,128)(2,1)S(1)} %get-tuple-element.21.m1_ref), channel_id=1, source_target_pairs={{0,31},{1,2},{2,1},{3,4},{4,3},{5,6},{6,5},{7,8},{8,7},{9,10},{10,... | collective-permute-start | bytes 786440 | tf_op jit(solution)/shard_map/ppermute | solution.py:32
  27.0 0.0 copy-done
  27.0 0.0 copy-done.1
  27.0 0.0 copy-done.3
  27.0 0.0 copy-done.4
  27.0 0.0 copy-done.5
  27.0 0.0 copy-done.6
  27.0 0.8 %matrix_weights.1 = (bf16[3584,256]{1,0:T(8,128)(2,1)S(1)}, bf16[4480,256]{1,0:T(8,128)(2,1)S(1)}, f32[8,256]{1,0:T(8,128)S(1)}) custom-call(bf16[49,32,64]{2,1,0:T(8,128)(2,1)S(1)} %bitcast.19, bf16[49,64,128]{2,1,0:T(8,128)(2,1)S(1)} %bitcast.18, f32[1,64]{1,0:T(1,128)S(1)} %bitcast.21, f32[1,64]{1,0:T(1,128)S(1)} %bitcast.22, f32[1,128]{1,0:T(1,128)S(1)} %bitcast.23, ...), custom_call_target="tpu_custom_call" | custom-call | bytes 8388608 | tf_op jit(solution)/shard_map/matrix_weights/pallas_call | solution.py:266
  27.9 0.0 collective-permute-done.2.ri0_ref
  27.9 3.9 %collective-permute-done.3.ri1_ref = bf16[32,32,128]{2,1,0:T(8,128)(2,1)S(1)} collective-permute-done((bf16[32,32,128]{2,1,0:T(8,128)(2,1)S(1)}, bf16[32,32,128]{2,1,0:T(8,128)(2,1)S(1)}, u32[]{:S(2)}, u32[]{:S(2)}) %collective-permute-start.3) | collective-permute-done | bytes 262176 | tf_op jit(solution)/shard_map/ppermute | solution.py:32
  31.8 0.9 %collective-permute-done.rb0_ref = bf16[32,32,128]{2,1,0:T(8,128)(2,1)S(1)} collective-permute-done((bf16[32,32,128]{2,1,0:T(8,128)(2,1)S(1)}, bf16[32,32,128]{2,1,0:T(8,128)(2,1)S(1)}, u32[]{:S(2)}, u32[]{:S(2)}) %collective-permute-start) | collective-permute-done | bytes 262176 | tf_op jit(solution)/shard_map/ppermute | solution.py:32
  32.7 5.7 %collective-permute-done.1.rb1_ref = bf16[32,32,128]{2,1,0:T(8,128)(2,1)S(1)} collective-permute-done((bf16[32,32,128]{2,1,0:T(8,128)(2,1)S(1)}, bf16[32,32,128]{2,1,0:T(8,128)(2,1)S(1)}, u32[]{:S(2)}, u32[]{:S(2)}) %collective-permute-start.1) | collective-permute-done | bytes 262176 | tf_op jit(solution)/shard_map/ppermute | solution.py:32
  38.4 5.0 %build_field.1 = (bf16[4,128,2,16,128]{4,3,2,1,0:T(8,128)(2,1)S(1)}, f32[7,272,128]{2,1,0:T(8,128)S(1)}, bf16[5,5,2,16,128]{4,3,2,1,0:T(8,128)(2,1)S(1)}, bf16[5,5,2,16,128]{4,3,2,1,0:T(8,128)(2,1)S(1)}) custom-call(f32[257,32,128]{2,1,0:T(8,128)S(1)} %get-tuple-element.19.acc, bf16[32,32,128]{2,1,0:T(8,128)(2,1)S(1)} %collective-permute-done.rb0_ref, ...), custom_call_target="tpu_custom_call" | custom-call | tf_op jit(solution)/shard_map/build_field/pallas_call | solution.py:365
  43.4 2.7 %collective-permute-start.4 = (bf16[5,5,2,16,128]{4,3,2,1,0:T(8,128)(2,1)S(1)}, bf16[5,5,2,16,128]{4,3,2,1,0:T(8,128)(2,1)S(1)}, u32[]{:S(2)}, u32[]{:S(2)}) collective-permute-start(bf16[5,5,2,16,128]{4,3,2,1,0:T(8,128)(2,1)S(1)} %get-tuple-element.28.ma_ref), channel_id=1, source_target_pairs={{0,16},{1,17},{2,18},{3,19},{4,20},{5,21},{6,22},{7,23},{8,24},{9,... | collective-permute-start | bytes 614408 | tf_op jit(solution)/shard_map/ppermute | solution.py:32
  46.2 0.0 collective-permute-start.5
  46.2 8.5 %first_conv.1.h_hbm = bf16[5,64,2,16,128]{4,3,2,1,0:T(8,128)(2,1)S(1)} custom-call(bf16[4,128,2,16,128]{4,3,2,1,0:T(8,128)(2,1)S(1)} %get-tuple-element.24.f_hbm, f32[7,272,128]{2,1,0:T(8,128)S(1)} %get-tuple-element.25.e_ref, bf16[3584,256]{1,0:T(8,128)(2,1)S(1)} %get-tuple-element.26.w_ref.w1_ref, f32[8,256]{1,0:T(8,128)S(1)} %get-tuple-element.27.v_ref), custom_call_target="tpu_custom_call" | custom-call | flops 4227858432 | bytes 12582912 | tf_op jit(solution)/shard_map/first_conv/pallas_call | solution.py:456
  54.7 0.0 collective-permute-done.4.ra_ref
  54.7 0.0 collective-permute-done.5.rb_ref
  54.7 7.0 %second_conv.1 = bf16[64,32,128]{2,1,0:T(8,128)(2,1)} custom-call(bf16[5,64,2,16,128]{4,3,2,1,0:T(8,128)(2,1)S(1)} %first_conv.1.h_hbm, bf16[5,5,2,16,128]{4,3,2,1,0:T(8,128)(2,1)S(1)} %get-tuple-element.28.ma_ref, bf16[5,5,2,16,128]{4,3,2,1,0:T(8,128)(2,1)S(1)} %get-tuple-element.29.mb_ref, bf16[5,5,2,16,128]{4,3,2,1,0:T(8,128)(2,1)S(1)} %collective-permute-done.4.ra_ref, ...), custom_call_target="tpu_custom_call" | custom-call | tf_op jit(solution)/shard_map/second_conv/pallas_call | solution.py:600
Async XLA Ops:
  0.0 4.8 %copy-start.2 = (s32[1,1,512]{2,1,0:T(1,128)S(1)}, s32[1,1,512]{2,1,0:T(1,128)}, u32[]{:S(2)}) copy-start(s32[1,1,512]{2,1,0:T(1,128)} %param.15) | copy-start | bytes 6148
  0.7 0.7 %copy-start.7 = (s32[1,1,128]{2,1,0:T(1,128)S(1)}, s32[1,1,128]{2,1,0:T(1,128)}, u32[]{:S(2)}) copy-start(s32[1,1,128]{2,1,0:T(1,128)} %param.19) | copy-start | bytes 1540
  4.8 22.2 %copy-start = (bf16[7,7,64,128]{3,2,1,0:T(8,128)(2,1)S(1)}, bf16[7,7,64,128]{3,2,1,0:T(8,128)(2,1)}, u32[]{:S(2)}) copy-start(bf16[7,7,64,128]{3,2,1,0:T(8,128)(2,1)} %param.23) | copy-start | bytes 2408452
  4.8 22.1 %copy-start.1 = (bf16[7,7,32,64]{3,2,1,0:T(8,128)(2,1)S(1)}, bf16[7,7,32,64]{3,2,1,0:T(8,128)(2,1)}, u32[]{:S(2)}) copy-start(bf16[7,7,32,64]{3,2,1,0:T(8,128)(2,1)} %param.20) | copy-start | bytes 602116
  4.9 22.1 %copy-start.3 = (f32[64]{0:T(128)S(1)}, f32[64]{0:T(128)}, u32[]{:S(2)}) copy-start(f32[64]{0:T(128)} %param.21) | copy-start | bytes 772
  4.9 22.1 %copy-start.4 = (f32[64]{0:T(128)S(1)}, f32[64]{0:T(128)}, u32[]{:S(2)}) copy-start(f32[64]{0:T(128)} %param.22) | copy-start | bytes 772
  4.9 22.1 %copy-start.5 = (f32[128]{0:T(128)S(1)}, f32[128]{0:T(128)}, u32[]{:S(2)}) copy-start(f32[128]{0:T(128)} %param.24) | copy-start | bytes 1540
  4.9 22.1 %copy-start.6 = (f32[128]{0:T(128)S(1)}, f32[128]{0:T(128)}, u32[]{:S(2)}) copy-start(f32[128]{0:T(128)} %param.25) | copy-start | bytes 1540
  16.5 11.4 %collective-permute-start.2 = (bf16[32,32,128]{2,1,0:T(8,128)(2,1)S(1)}, bf16[32,32,128]{2,1,0:T(8,128)(2,1)S(1)}, u32[]{:S(2)}, u32[]{:S(2)}) collective-permute-start(bf16[32,32,128]{2,1,0:T(8,128)(2,1)S(1)} %get-tuple-element.22), channel_id=1, source_target_pairs={{0,1},{1,0},{2,3},{3,2},{4,5},{5,4},{6,7},{7,6},{8,9},{9,8},{10,11... | collective-permute-start | bytes 786440 | tf_op jit(solution)/shard_map/ppermute | solution.py:32
  18.7 13.1 %collective-permute-start.3 = (bf16[32,32,128]{2,1,0:T(8,128)(2,1)S(1)}, bf16[32,32,128]{2,1,0:T(8,128)(2,1)S(1)}, u32[]{:S(2)}, u32[]{:S(2)}) collective-permute-start(bf16[32,32,128]{2,1,0:T(8,128)(2,1)S(1)} %get-tuple-element.23), channel_id=1, source_target_pairs={{0,31},{1,2},{2,1},{3,4},{4,3},{5,6},{6,5},{7,8},{8,7},{9,10},{10,... | collective-permute-start | bytes 786440 | tf_op jit(solution)/shard_map/ppermute | solution.py:32
  26.1 6.6 %collective-permute-start = (bf16[32,32,128]{2,1,0:T(8,128)(2,1)S(1)}, bf16[32,32,128]{2,1,0:T(8,128)(2,1)S(1)}, u32[]{:S(2)}, u32[]{:S(2)}) collective-permute-start(bf16[32,32,128]{2,1,0:T(8,128)(2,1)S(1)} %get-tuple-element.20.m0_ref), channel_id=1, source_target_pairs={{0,1},{1,0},{2,3},{3,2},{4,5},{5,4},{6,7},{7,6},{8,9},{9,8},{10,11... | collective-permute-start | bytes 786440 | tf_op jit(solution)/shard_map/ppermute | solution.py:32
  26.1 12.3 %collective-permute-start.1 = (bf16[32,32,128]{2,1,0:T(8,128)(2,1)S(1)}, bf16[32,32,128]{2,1,0:T(8,128)(2,1)S(1)}, u32[]{:S(2)}, u32[]{:S(2)}) collective-permute-start(bf16[32,32,128]{2,1,0:T(8,128)(2,1)S(1)} %get-tuple-element.21.m1_ref), channel_id=1, source_target_pairs={{0,31},{1,2},{2,1},{3,4},{4,3},{5,6},{6,5},{7,8},{8,7},{9,10},{10,... | collective-permute-start | bytes 786440 | tf_op jit(solution)/shard_map/ppermute | solution.py:32
  43.4 11.2 %collective-permute-start.4 = (bf16[5,5,2,16,128]{4,3,2,1,0:T(8,128)(2,1)S(1)}, bf16[5,5,2,16,128]{4,3,2,1,0:T(8,128)(2,1)S(1)}, u32[]{:S(2)}, u32[]{:S(2)}) collective-permute-start(bf16[5,5,2,16,128]{4,3,2,1,0:T(8,128)(2,1)S(1)} %get-tuple-element.28.ma_ref), channel_id=1, source_target_pairs={{0,16},{1,17},{2,18},{3,19},{4,20},{5,21},{6,22},{7,23},{8,24},{9,... | collective-permute-start | bytes 614408 | tf_op jit(solution)/shard_map/ppermute | solution.py:32
  46.2 8.5 %collective-permute-start.5 = (bf16[5,5,2,16,128]{4,3,2,1,0:T(8,128)(2,1)S(1)}, bf16[5,5,2,16,128]{4,3,2,1,0:T(8,128)(2,1)S(1)}, u32[]{:S(2)}, u32[]{:S(2)}) collective-permute-start(bf16[5,5,2,16,128]{4,3,2,1,0:T(8,128)(2,1)S(1)} %get-tuple-element.29.mb_ref), channel_id=1, source_target_pairs={{0,32},{1,33},{2,34},{3,35},{4,36},{5,37},{6,38},{7,39},{8,40},{9,... | collective-permute-start | bytes 614408 | tf_op jit(solution)/shard_map/ppermute | solution.py:32

commit v2 on v1

v2 whole, which is shorter than its diff:
```python
import jax
import jax.numpy as jnp
from jax import lax
from jax.experimental import pallas as pl
from jax.experimental.pallas import tpu as pltpu
from jax.sharding import PartitionSpec as P

F32 = jnp.float32
BF16 = jnp.bfloat16
BANDS = 4
SECTORS = 32
BIG = 24 << 20


def mesh_pairs(partner):
    return [
        (b * SECTORS + s, (lambda t: t[0] * SECTORS + t[1] % SECTORS)(partner(b, s)))
        for b in range(BANDS)
        for s in range(SECTORS)
    ]


LON_EVEN = mesh_pairs(lambda b, s: (b, s ^ 1))
LON_ODD = mesh_pairs(lambda b, s: (b, s + 1 if s % 2 else s - 1))
LAT_OUTER = mesh_pairs(
    lambda b, s: {0: (0, s + 16), 1: (2, s), 2: (1, s), 3: (3, s + 16)}[b]
)
LAT_INNER = mesh_pairs(lambda b, s: (b ^ 1, s))


def exchange(block, pairs):
    return lax.ppermute(block, ("lat", "lon"), pairs)


def nt_dot(a, b):
    return lax.dot_general(a, b, (((1,), (1,)), ((), ())), preferred_element_type=F32)


def group_ones(size, width):
    rows = lax.broadcasted_iota(jnp.int32, (size, size), 0) // width
    cols = lax.broadcasted_iota(jnp.int32, (size, size), 1) // width
    return (rows == cols).astype(F32).astype(BF16)


def norm_gelu(v, gain, ones, width):
    sq = v * v
    hi = sq.astype(BF16)
    lo = (sq - hi.astype(F32)).astype(BF16)
    total = jnp.dot(hi, ones, preferred_element_type=F32)
    total = total + jnp.dot(lo, ones, preferred_element_type=F32)
    x = v * lax.rsqrt(total * (1.0 / width) + 1e-05) * gain
    return jax.nn.gelu(x, approximate=True)


def unit(size):
    rows = lax.broadcasted_iota(jnp.int32, (size, size), 0)
    cols = lax.broadcasted_iota(jnp.int32, (size, size), 1)
    return (rows == cols).astype(F32).astype(BF16)


HBM = pl.BlockSpec(memory_space=pltpu.HBM)
SMEM = pl.BlockSpec(memory_space=pltpu.SMEM)
VMEM = pl.BlockSpec(memory_space=pltpu.VMEM)


def in_hbm(x):
    return pltpu.with_memory_space_constraint(x, pltpu.HBM)


def half_lanes():
    lanes = lax.broadcasted_iota(jnp.int32, (16, 128), 1)
    low = (lanes < 64).astype(F32).astype(BF16)
    high = (lanes >= 64).astype(F32).astype(BF16)
    return low, high


def send_sides(m0_ref, m1_ref, east, west):
    odd = lax.axis_index("lon") % 2

    def fill(east_ref, west_ref):
        for q in range(32):
            east_ref[q] = east(q).astype(BF16)
            west_ref[q] = west(q).astype(BF16)

    @pl.when(odd == 0)
    def _():
        fill(m0_ref, m1_ref)

    @pl.when(odd == 1)
    def _():
        fill(m1_ref, m0_ref)


def border_kernel(btarget, x_hbm, w_hbm, m0_ref, m1_ref, token, xv, wv, st, sb, acc, sem):
    states = pltpu.make_async_copy(x_hbm, xv, sem.at[4])
    states.start()
    chunks = [
        pltpu.make_async_copy(
            w_hbm.at[pl.ds(32 * c, 32)], wv.at[pl.ds(32 * c, 32)], sem.at[c]
        )
        for c in range(4)
    ]
    for c in chunks:
        c.start()
    acc[...] = jnp.zeros_like(acc)
    low, high = half_lanes()
    eye = unit(128)
    states.wait()
    for c in range(0, 16, 2):
        x = jnp.concatenate([xv[c], xv[c + 16], xv[c + 1], xv[c + 17]], axis=0)
        out = nt_dot(eye, x)
        st[pl.ds(c, 128, stride=16), :] = out[:, :128]
        st[pl.ds(c + 1, 128, stride=16), :] = out[:, 128:]
    for q in range(8):
        sb[16 * q : 16 * q + 16] = st[256 * q : 256 * q + 256].astype(BF16).reshape(16, 16, 128)
    for c in range(4):
        chunks[c].wait()

        def body(carry, c=c):
            n0 = 32 * c
            vals = []
            for u in range(0, 32, 2):
                rows = [sb[n0 + u + k] * half for k in range(2) for half in (low, high)]
                w = jnp.concatenate([wv[n0 + u], wv[n0 + u + 1]], axis=1)
                rhs = jnp.concatenate([w, w], axis=0)
                vals.append(
                    jnp.dot(jnp.concatenate(rows, axis=0), rhs, preferred_element_type=F32)
                )
            for u in range(32):
                k = u % 2
                acc[btarget[n0 + u]] += vals[u // 2][32 * k : 32 * k + 32, 128 * k : 128 * k + 128]
            return carry

        body(0)
    send_sides(m0_ref, m1_ref, lambda q: acc[32 + q], lambda q: acc[q])
    token[...] = jnp.zeros_like(token)


def border_sums(btarget, bstate, bweight):
    side = jax.ShapeDtypeStruct((32, 32, 128), BF16)
    return pl.pallas_call(
        border_kernel,
        name="border_sums",
        in_specs=[SMEM, HBM, HBM],
        out_specs=[VMEM, VMEM, VMEM],
        out_shape=[side, side, jax.ShapeDtypeStruct((8, 128), F32)],
        scratch_shapes=[
            pltpu.VMEM((32, 64, 128), BF16),
            pltpu.VMEM((128, 64, 128), BF16),
            pltpu.VMEM((2048, 128), F32),
            pltpu.VMEM((128, 16, 128), BF16),
            pltpu.VMEM((64, 32, 128), F32),
            pltpu.SemaphoreType.DMA((5,)),
        ],
        cost_estimate=pl.CostEstimate(
            flops=2 * 128 * 32 * 64 * 128, bytes_accessed=4 << 20, transcendentals=0
        ),
        compiler_params=pltpu.CompilerParams(vmem_limit_bytes=BIG),
    )(btarget, in_hbm(jnp.transpose(bstate, (1, 2, 0))), in_hbm(bweight))


def sums_kernel(
    target, count, after, x_hbm, w_hbm, acc_ref, m0_ref, m1_ref, xv, wv, st, sb, xsem, wsem
):
    states = [
        pltpu.make_async_copy(x_hbm.at[:, :, pl.ds(256 * p, 256)], xv.at[p], xsem.at[p])
        for p in range(2)
    ]
    chunks = {
        (p, c, h): pltpu.make_async_copy(
            w_hbm.at[pl.ds(256 * p + 128 * h + 32 * c, 32)],
            wv.at[pl.ds(256 * p + 128 * h + 32 * c, 32)],
            wsem.at[p, c, h],
        )
        for p in range(2)
        for c in range(4)
        for h in range(2)
    }
    for p in range(2):
        states[p].start()
    for c in chunks.values():
        c.start()
    low, high = half_lanes()
    low = jnp.concatenate([low, low], axis=0)
    high = jnp.concatenate([high, high], axis=0)
    eye = unit(128)
    for p in range(2):
        states[p].wait()
        for c in range(0, 32, 2):
            x = jnp.concatenate(
                [xv[p, c + k, :, 128 * h : 128 * h + 128] for k in range(2) for h in range(2)], axis=0
            )
            out = nt_dot(eye, x)
            st[pl.ds(c, 128, stride=32), :] = out[:, :128]
            st[pl.ds(c + 1, 128, stride=32), :] = out[:, 128:]
        for q in range(16):
            sb[128 * p + 8 * q : 128 * p + 8 * q + 8] = (
                st[256 * q : 256 * q + 256].astype(BF16).reshape(8, 32, 128)
            )
    for p in range(2):
        for c in range(4):
            for h in range(2):
                chunks[p, c, h].wait()
        for u in range(0, 128, 2):
            rows = [sb[128 * p + u + k] * half for k in range(2) for half in (low, high)]
            cols = [[wv[256 * p + 128 * h + u + k] for k in range(2)] for h in range(2)]
            rhs = jnp.concatenate([jnp.concatenate(r, axis=1) for r in cols], axis=0)
            both = jnp.dot(jnp.concatenate(rows, axis=0), rhs, preferred_element_type=F32)
            for k in range(2):
                for h in range(2):
                    n = 256 * p + 128 * h + u + k
                    at = 64 * k + 32 * h
                    v = both[at : at + 32, 128 * k : 128 * k + 128]
                    if p == 0:
                        acc_ref[target[n]] = v
                    else:
                        acc_ref[jnp.where(n < count[0], target[n], 256)] += v
    send_sides(m0_ref, m1_ref, lambda q: acc_ref[8 * q + 7], lambda q: acc_ref[8 * q])


def inner_sums(target, count, after, state, weight):
    side = jax.ShapeDtypeStruct((32, 32, 128), BF16)
    return pl.pallas_call(
        sums_kernel,
        name="inner_sums",
        in_specs=[SMEM, SMEM, VMEM, HBM, HBM],
        out_specs=[VMEM, VMEM, VMEM],
        out_shape=[pltpu.VMEM((257, 32, 128), F32), side, side],
        scratch_shapes=[
            pltpu.VMEM((2, 32, 64, 256), BF16),
            pltpu.VMEM((512, 64, 128), BF16),
            pltpu.VMEM((4096, 128), F32),
            pltpu.VMEM((256, 32, 128), BF16),
            pltpu.SemaphoreType.DMA((2,)),
            pltpu.SemaphoreType.DMA((2, 4, 2)),
        ],
        cost_estimate=pl.CostEstimate(
            flops=2 * 512 * 32 * 64 * 128, bytes_accessed=16 << 20, transcendentals=0
        ),
        compiler_params=pltpu.CompilerParams(vmem_limit_bytes=BIG),
    )(target, count, after, in_hbm(jnp.transpose(state, (1, 2, 0))), in_hbm(weight))


def weights_kernel(k1_ref, k2_ref, b1_ref, g1_ref, b2_ref, g2_ref, w1_ref, w2_ref, v_ref):
    w1_ref[...] = jnp.zeros_like(w1_ref)
    w2_ref[...] = jnp.zeros_like(w2_ref)
    for r in range(7):
        for s in range(7):
            for t in range(4):
                row = r * 512 + (2 * t + s + 1) * 32
                w1_ref[row : row + 32, t * 64 : (t + 1) * 64] = k1_ref[r * 7 + s]
            for t in range(2):
                row = r * 640 + (2 * t + s + 1) * 64
                w2_ref[row : row + 64, t * 128 : (t + 1) * 128] = k2_ref[r * 7 + s]
    for t in range(4):
        v_ref[0:1, t * 64 : (t + 1) * 64] = b1_ref[...]
        v_ref[1:2, t * 64 : (t + 1) * 64] = g1_ref[...]
    for t in range(2):
        v_ref[2:3, t * 128 : (t + 1) * 128] = b2_ref[...]
        v_ref[3:4, t * 128 : (t + 1) * 128] = g2_ref[...]


def matrix_weights(k1, k2, b1, g1, b2, g2):
    return pl.pallas_call(
        weights_kernel,
        name="matrix_weights",
        out_shape=[
            jax.ShapeDtypeStruct((3584, 256), BF16),
            jax.ShapeDtypeStruct((4480, 256), BF16),
            jax.ShapeDtypeStruct((8, 256), F32),
        ],
        cost_estimate=pl.CostEstimate(flops=0, bytes_accessed=8 << 20, transcendentals=0),
        compiler_params=pltpu.CompilerParams(vmem_limit_bytes=16 << 20),
    )(k1.reshape(49, 32, 64), k2.reshape(49, 64, 128), b1[None], g1[None], b2[None], g2[None])


def field_kernel(
    acc, rb0_ref, rb1_ref, ri0_ref, ri1_ref, m0_ref, m1_ref, f_ref, e_ref, ma_ref, mb_ref, fs, et
):
    odd = lax.axis_index("lon") % 2
    upper = lax.axis_index("lat") % 2
    rows = lax.broadcasted_iota(jnp.int32, (32, 128), 0)
    pix = lax.broadcasted_iota(jnp.int32, (32, 128), 1)
    pick = (pix // 4 == (rows % 8) * 4 + rows // 8).astype(F32).astype(BF16)
    keep = (
        lax.broadcasted_iota(jnp.int32, (128, 128), 0) // 32
        == lax.broadcasted_iota(jnp.int32, (128, 128), 1) % 4
    ).astype(F32).astype(BF16)
    f_ref[:, 0:2] = jnp.zeros((4, 2, 2, 16, 128), BF16)
    f_ref[:, 130:132] = jnp.zeros((4, 2, 2, 16, 128), BF16)
    et[...] = jnp.zeros_like(et)
    is_odd = odd == 1

    def step(i, carry):
        for y in range(4):
            east_border = jnp.where(is_odd, rb1_ref[4 * i + y], rb0_ref[4 * i + y]).astype(F32)
            east_inner = jnp.where(is_odd, ri1_ref[4 * i + y], ri0_ref[4 * i + y]).astype(F32)
            west_border = jnp.where(is_odd, rb0_ref[4 * i + y], rb1_ref[4 * i + y]).astype(F32)
            west_inner = jnp.where(is_odd, ri0_ref[4 * i + y], ri1_ref[4 * i + y]).astype(F32)
            own_east = jnp.where(is_odd, m1_ref[4 * i + y], m0_ref[4 * i + y]).astype(F32)
            own_west = jnp.where(is_odd, m0_ref[4 * i + y], m1_ref[4 * i + y]).astype(F32)
            patches = [acc[32 * i + 8 * y + c] for c in range(8)]
            patches[0] = patches[0] + west_border
            patches[7] = patches[7] + east_border
            patches = [west_inner + own_west] + patches + [east_inner + own_east]
            for c in range(0, 10, 2):
                pair = [patches[c].astype(BF16), patches[c + 1].astype(BF16)]
                spread = jnp.concatenate(
                    [jnp.concatenate([v] * 4, axis=0) * keep for v in pair], axis=0
                )
                both = nt_dot(pick, spread)
                for h in range(2):
                    pc = c + h - 1
                    for k in range(4):
                        v = both[8 * k : 8 * k + 8, 128 * h : 128 * h + 128]
                        g = 2 * pc + k // 2
                        kk = 4 * pc + k
                        if 0 <= pc < 8:
                            fs[y, k % 2, pl.ds(g, 8, stride=16), :] = v
                        if k % 2 == 0 and 1 <= g <= 16:
                            fs[y, 3, pl.ds(g - 1, 8, stride=16), :] = v
                        if k % 2 == 1 and -1 <= g <= 14:
                            fs[y, 2, pl.ds(g + 1, 8, stride=16), :] = v
                        if kk in (-3, -2, -1, 0, 31, 32, 33):
                            slot = kk + 3 if kk <= 0 else kk - 27
                            e_ref[slot, pl.ds(8 + 32 * i + 8 * y, 8), :] = v
                            et[y, pl.ds(slot, 8, stride=16), :] = v
            for a in range(4):
                f_ref[a, pl.ds(2 + 16 * i + 4 * y, 4)] = fs[y, a].astype(BF16).reshape(4, 2, 16, 128)

        def send(ref, first, start):
            for a in range(4):
                ref[a] = f_ref[a, 2 + start + first : 2 + start + first + 5]
            for q in range(5):
                y, o = (first + q) // 4, (first + q) % 4
                ref[4, q] = et[y, 32 * o : 32 * o + 32].astype(BF16).reshape(2, 16, 128)

        @pl.when((i == 0) & (upper == 0))
        def _():
            send(ma_ref, 0, 0)

        @pl.when((i == 0) & (upper == 1))
        def _():
            send(mb_ref, 0, 0)

        @pl.when((i == 7) & (upper == 0))
        def _():
            send(mb_ref, 11, 112)

        @pl.when((i == 7) & (upper == 1))
        def _():
            send(ma_ref, 11, 112)

        return carry

    lax.fori_loop(0, 8, step, 0)


def build_field(acc, *sides):
    msg = jax.ShapeDtypeStruct((5, 5, 2, 16, 128), BF16)
    return pl.pallas_call(
        field_kernel,
        name="build_field",
        in_specs=[VMEM] * 7,
        out_specs=[VMEM] * 4,
        out_shape=[
            pltpu.VMEM((4, 132, 2, 16, 128), BF16),
            pltpu.VMEM((7, 272, 128), F32),
            msg,
            msg,
        ],
        scratch_shapes=[
            pltpu.VMEM((4, 4, 128, 128), F32),
            pltpu.VMEM((4, 128, 128), F32),
        ],
        compiler_params=pltpu.CompilerParams(vmem_limit_bytes=24 << 20),
    )(acc, *sides)


ORDER = (2, 0, 1, 3)


TILE = 32


def first_kernel(f_ref, e_ref, w_ref, v_ref, h_ref, raw, edge, hs, ms, el):
    ones = group_ones(256, 64)
    many = TILE * 16
    tiles = 128 // TILE

    def mix(lhs):
        return jnp.dot(lhs, w_ref[...], preferred_element_type=F32) + v_ref[0:1]

    def side(n):
        parts = []
        for r in range(7):
            for j in range(4):
                slot = 4 * n + j
                if slot == 7:
                    parts.append(jnp.zeros((128, 128), BF16))
                else:
                    parts.append(e_ref[slot, pl.ds(8 - 3 + r, 128, stride=2), :].astype(BF16))
        return jnp.concatenate(parts, axis=1)

    def start(i):
        parts = []
        for r in range(7):
            for a in ORDER:
                first = TILE * i + (r + 1) // 2
                x = f_ref[a, first : first + TILE, (r + 1) % 2]
                parts.append(x.reshape(many, 128))
        raw[i] = mix(jnp.concatenate(parts, axis=1))

    def finish(i):
        h = norm_gelu(raw[i], v_ref[1:2], ones, 64)
        for c in range(2):
            hs[i, c, 8 : 8 + many] = h[:, 128 * c : 128 * c + 128]
        ms[i, 0] = hs[i, 0, 7 : 7 + many]
        ms[i, 1] = hs[i, 1, 7 : 7 + many]
        ms[i, 2] = hs[i, 0, 9 : 9 + many]
        rows = slice(TILE * i, TILE * i + TILE)
        ms[i, 0, pl.ds(0, TILE, stride=16), :] = el[0, rows, 0:128]
        ms[i, 1, pl.ds(0, TILE, stride=16), :] = el[0, rows, 128:256]
        ms[i, 2, pl.ds(15, TILE, stride=16), :] = el[1, rows, 0:128]
        half = TILE // 2
        tile = lambda v: v.astype(BF16).reshape(half, 2, 16, 128)
        to = slice(half * i, half * i + half)
        h_ref[0, to] = tile(ms[i, 0])
        h_ref[1, to] = tile(ms[i, 1])
        h_ref[2, to] = tile(hs[i, 0, 8 : 8 + many])
        h_ref[3, to] = tile(hs[i, 1, 8 : 8 + many])
        h_ref[4, to] = tile(ms[i, 2])

    edge[...] = mix(jnp.concatenate([side(0), side(1)], axis=0))
    start(0)
    out = norm_gelu(edge[...], v_ref[1:2], ones, 64)
    el[0] = out[0:128]
    el[1] = out[128:256]
    for i in range(tiles):
        if i + 1 < tiles:
            start(i + 1)
        finish(i)


def first_conv(f, e, w1, vec):
    tiles = 128 // TILE
    many = TILE * 16
    return pl.pallas_call(
        first_kernel,
        name="first_conv",
        in_specs=[VMEM] * 4,
        out_specs=VMEM,
        out_shape=pltpu.VMEM((5, 64, 2, 16, 128), BF16),
        scratch_shapes=[
            pltpu.VMEM((tiles, many, 256), F32),
            pltpu.VMEM((256, 256), F32),
            pltpu.VMEM((tiles, 2, many + 16, 128), F32),
            pltpu.VMEM((tiles, 3, many, 128), F32),
            pltpu.VMEM((2, 128, 256), F32),
        ],
        cost_estimate=pl.CostEstimate(
            flops=2 * 2304 * 3584 * 256, bytes_accessed=12 << 20, transcendentals=1 << 20
        ),
        compiler_params=pltpu.CompilerParams(vmem_limit_bytes=28 << 20),
    )(f, e, w1, vec)


BASES = (0, 2, 4, 11, 13, 20, 27, 29)


def second_kernel(
    h_ref, ma_ref, mb_ref, ra_ref, rb_ref, w1_ref, w2_ref, v_ref,
    o_ref, top, bot, ve, vf, le, ts, ms, raw, os,
):
    lat = lax.axis_index("lat")
    odd = lat % 2 == 1
    north = lat == 0
    south = lat == 3
    ones1 = group_ones(256, 64)
    ones2 = group_ones(256, 128)

    def window(ref, first, count):
        parts = []
        for r in range(7):
            for a in range(5):
                at = first + (r + 1) // 2
                parts.append(ref[a, at : at + count, (r + 1) % 2].reshape(16 * count, 128))
        return jnp.concatenate(parts, axis=1)

    def mix(lhs):
        return jnp.dot(lhs, w2_ref[...], preferred_element_type=F32) + v_ref[2:3]

    def finish(n, at, first, count):
        y = norm_gelu(raw[n, at : at + 16 * count], v_ref[3:4], ones2, 128)
        for t in range(2):
            os[n, pl.ds(2 * at + t, 16 * count, stride=2), :] = y[:, 128 * t : 128 * t + 128]
        o_ref[first : first + count] = (
            os[n, 2 * at : 2 * at + 32 * count].astype(BF16).reshape(count, 32, 128)
        )

    def row(ref, a, m):
        return ref[a, m // 2, m % 2]

    def own_top(a, m):
        return jnp.where(odd, row(mb_ref, a, m), row(ma_ref, a, m))

    def own_bot(a, m):
        return jnp.where(odd, row(ma_ref, a, m), row(mb_ref, a, m))

    def halo_top(a, m):
        return jnp.where(odd, row(rb_ref, a, m), row(ra_ref, a, m))

    def halo_bot(a, m):
        return jnp.where(odd, row(ra_ref, a, m), row(rb_ref, a, m))

    for a in range(5):
        def put(n, v):
            if a < 4:
                vf[a, n] = v
            else:
                ve[16 * n : 16 * n + 16] = v.astype(F32)

        for q in range(11):
            normal = halo_top(a, q + 1) if q < 9 else own_top(a, q - 9)
            polar = own_top(a, 2 - q) if q < 3 else halo_top(a, q - 3)
            put(q, jnp.where(north, polar, normal))
        for q in range(9):
            if q < 3:
                v = jnp.where(north, halo_top(a, 2 - q), halo_top(a, 7 + q))
            else:
                v = own_top(a, q - 3)
            put(11 + q, v)
        for q in range(7):
            if q < 5:
                v = own_bot(a, 5 + q)
            else:
                v = jnp.where(south, halo_bot(a, 14 - q), halo_bot(a, q - 5))
            put(20 + q, v)
        for q in range(9):
            normal = own_bot(a, 7 + q) if q < 3 else halo_bot(a, q - 3)
            polar = halo_bot(a, 3 + q) if q < 7 else own_bot(a, 16 - q)
            put(27 + q, jnp.where(south, polar, normal))

    for n, base in enumerate(BASES):
        for r in range(7):
            for j in range(4):
                col = 128 * (4 * r + j)
                for side in range(2):
                    src = 16 * (base + r) + 4 * side + j
                    le[n + 8 * side : n + 8 * side + 1, col : col + 128] = ve[src : src + 1, :]
    parts = []
    for r in range(7):
        for a in ORDER:
            parts.append(jnp.concatenate([vf[a, base + r] for base in BASES], axis=0))
    lhs = jnp.concatenate([jnp.concatenate(parts, axis=1), le[...].astype(BF16)], axis=0)
    ts[2] = jnp.dot(lhs, w1_ref[...], preferred_element_type=F32) + v_ref[0:1]
    raw[0] = mix(window(h_ref, 14, 32))
    for a in range(5):
        top[a, 2:20] = h_ref[a, 0:18]
        bot[a, 0:18] = h_ref[a, 46:64]
    h = norm_gelu(ts[2], v_ref[1:2], ones1, 64)
    for c in range(2):
        ts[c, 8:136, 0:128] = h[0:128, 128 * c : 128 * c + 128]
    ms[0] = ts[0, 7:135, 0:128]
    ms[1] = ts[1, 7:135, 0:128]
    ms[2] = ts[0, 9:137, 0:128]
    ms[0, pl.ds(0, 8, stride=16), :] = h[128:136, 0:128]
    ms[1, pl.ds(0, 8, stride=16), :] = h[128:136, 128:256]
    ms[2, pl.ds(15, 8, stride=16), :] = h[136:144, 0:128]
    full = [ms[0], ms[1], ts[0, 8:136, 0:128], ts[1, 8:136, 0:128], ms[2]]
    for a in range(5):
        v = full[a].astype(BF16).reshape(8, 16, 128)
        top[a, 0, 1] = jnp.where(north, v[2], v[0])
        top[a, 1, 0] = v[1]
        top[a, 1, 1] = jnp.where(north, v[0], v[2])
        top[a, 2, 0] = v[3]
        top[a, 2, 1] = v[4]
        bot[a, 17, 1] = v[5]
        bot[a, 18, 0] = jnp.where(south, v[7], v[6])
        bot[a, 18, 1] = jnp.where(south, v[6], v[7])
    raw[1] = mix(jnp.concatenate([window(top, 0, 16), window(bot, 0, 16)], axis=0))
    finish(0, 0, 16, 32)
    finish(1, 0, 0, 16)
    finish(1, 256, 48, 16)


def second_conv(h, ma, mb, ra, rb, w1, w2, vec):
    return pl.pallas_call(
        second_kernel,
        name="second_conv",
        in_specs=[VMEM] * 8,
        out_specs=VMEM,
        out_shape=jax.ShapeDtypeStruct((64, 32, 128), BF16),
        scratch_shapes=[
            pltpu.VMEM((5, 20, 2, 16, 128), BF16),
            pltpu.VMEM((5, 20, 2, 16, 128), BF16),
            pltpu.VMEM((36 * 16, 128), F32),
            pltpu.VMEM((4, 36, 16, 128), BF16),
            pltpu.VMEM((16, 3584), F32),
            pltpu.VMEM((3, 144, 256), F32),
            pltpu.VMEM((3, 128, 128), F32),
            pltpu.VMEM((2, 512, 256), F32),
            pltpu.VMEM((2, 1024, 128), F32),
        ],
        compiler_params=pltpu.CompilerParams(vmem_limit_bytes=28 << 20),
    )(h, ma, mb, ra, rb, w1, w2, vec)


def local(
    cell_state,
    remap_weight,
    block_target,
    block_count,
    border_state,
    border_weight,
    border_target,
    kernel_one,
    bias_one,
    gain_one,
    kernel_two,
    bias_two,
    gain_two,
):
    m0, m1, after = border_sums(border_target[0, 0], border_state[0, 0], border_weight[0, 0])
    rb0 = exchange(m0, LON_EVEN)
    rb1 = exchange(m1, LON_ODD)
    acc, i0, i1 = inner_sums(
        block_target[0, 0], block_count[0], after, cell_state[0, 0], remap_weight[0, 0]
    )
    ri0 = exchange(i0, LON_EVEN)
    ri1 = exchange(i1, LON_ODD)
    w1, w2, vec = matrix_weights(kernel_one, kernel_two, bias_one, gain_one, bias_two, gain_two)
    f, e, ma, mb = build_field(acc, rb0, rb1, ri0, ri1, m0, m1)
    ra = exchange(ma, LAT_OUTER)
    rb = exchange(mb, LAT_INNER)
    h = first_conv(f, e, w1, vec)
    return second_conv(h, ma, mb, ra, rb, w1, w2, vec)


def solution(mesh):
    placed = (
        P("lat", "lon", None, None, None),
        P("lat", "lon", None, None, None),
        P("lat", "lon", None),
        P("lat", "lon"),
        P("lat", "lon", None, None, None),
        P("lat", "lon", None, None, None),
        P("lat", "lon", None),
        P(),
        P(),
        P(),
        P(),
        P(),
        P(),
    )
    return jax.shard_map(
        local, mesh=mesh, in_specs=placed, out_specs=P("lat", "lon", None), check_vma=False
    )
```

time: 62 us -> 56.8 us (0.916)
  Pallas kernels: 36.4 us -> 31.4 us
    pallas_call x3, Pallas kernels: 20.5 us -> 16.2 us  [the longest x1 6.27 us: first_conv(): pl.pallas_call(first_kernel, name='first_conv', in_specs=[VMEM] * 4, out_...]
    pallas_call x1, Pallas kernels: 11.6 us -> 10.8 us  [inner_sums(): pl.pallas_call(sums_kernel, name='inner_sums', in_specs=[SMEM, SMEM, VMEM...]
  transfers between devices with their start and end apart: 6 -> 6, of which waited for: 3 -> 3; matrix products, arithmetic and copies ran while one was open for 0% -> 0% of each run, Pallas kernels for 15% -> 13%
where the time goes in v2:
time: 56.8 us; the launch traced here: 56.6 us
  Pallas kernels  31.4 us (55%)
  starting transfers between devices  13.3 us (23%)
  waiting for transfers between devices  10.5 us (18%)
  between operations  0.82 us (1%)
  local copies, waits for them, and re-layouts  0.69 us (1%)
    ppermute x6, starting transfers between devices, exchange(): return lax.ppermute(block, ('lat', 'lon'), pairs)  13.3 us
    pallas_call x1, Pallas kernels, inner_sums(): pl.pallas_call(sums_kernel, name='inner_sums', in_specs=[SMEM, SMEM, VMEM...  10.8 us
    ppermute x6, waiting for transfers between devices, exchange(): return lax.ppermute(block, ('lat', 'lon'), pairs)  10.5 us
    pallas_call x1, Pallas kernels, first_conv(): pl.pallas_call(first_kernel, name='first_conv', in_specs=[VMEM] * 4, out_...  6.27 us
    pallas_call x1, Pallas kernels, second_conv(): pl.pallas_call(second_kernel, name='second_conv', in_specs=[VMEM] * 8, ou...  5.11 us
    pallas_call x1, Pallas kernels, build_field(): pl.pallas_call(field_kernel, name='build_field', in_specs=[VMEM] * 7, out...  4.86 us
    pallas_call x1, Pallas kernels, border_sums(): pl.pallas_call(border_kernel, name='border_sums', in_specs=[SMEM, HBM, HB...  3.49 us
  transfers between devices with their start and end apart: 6, of which 3 were waited for; matrix products, arithmetic and copies ran while one was open for 0% of the time, Pallas kernels for 13%

profile of v2, /device:TPU:1, one launch (start us, length us, event | category | flops | bytes accessed | tf_op | source)
XLA Modules:
  0.0 56.6 jit_solution(4654597080105271110)
XLA Ops:
  0.0 0.0 copy-start.2
  0.7 0.0 copy-start.7
  0.7 0.6 %copy-done.7 = s32[1,1,128]{2,1,0:T(1,128)S(1)} copy-done((s32[1,1,128]{2,1,0:T(1,128)S(1)}, s32[1,1,128]{2,1,0:T(1,128)}, u32[]{:S(2)}) %copy-start.7) | copy-done | bytes 536
  1.3 3.5 %border_sums.1 = (bf16[32,32,128]{2,1,0:T(8,128)(2,1)S(1)}, bf16[32,32,128]{2,1,0:T(8,128)(2,1)S(1)}, f32[8,128]{1,0:T(8,128)S(1)}) custom-call(s32[128]{0:T(128)S(1)} %bitcast.25, bf16[32,64,128]{2,1,0:T(8,128)(2,1)} %bitcast.29, bf16[128,64,128]{2,1,0:T(8,128)(2,1)} %bitcast.27), custom_call_target="tpu_custom_call" | custom-call | flops 67108864 | bytes 4194304 | tf_op jit(solution)/shard_map/border_sums/pallas_call | solution.py:141
  4.8 0.0 copy-done.2
  4.8 0.0 copy-start
  4.8 0.0 copy-start.1
  4.9 0.0 copy-start.3
  4.9 0.0 copy-start.4
  4.9 0.0 copy-start.5
  4.9 0.0 copy-start.6
  4.9 10.8 %inner_sums.1 = (f32[257,32,128]{2,1,0:T(8,128)S(1)}, bf16[32,32,128]{2,1,0:T(8,128)(2,1)S(1)}, bf16[32,32,128]{2,1,0:T(8,128)(2,1)S(1)}) custom-call(s32[512]{0:T(512)S(1)} %bitcast.20, s32[1]{0:T(128)} %bitcast.17.count, f32[8,128]{1,0:T(8,128)S(1)} %get-tuple-element.18.after, bf16[32,64,512]{2,1,0:T(8,128)(2,1)} %bitcast.28, bf16[512,64,128]{2,1,0:T(8,128)(2,1)} %bitcast.26), custom_call_target="tpu_custom_call" | custom-call | flops 268435456 | bytes 16777216 | tf_op jit(solution)/shard_map/inner_sums/pallas_call | solution.py:223
  15.7 2.1 %collective-permute-start.2 = (bf16[32,32,128]{2,1,0:T(8,128)(2,1)S(1)}, bf16[32,32,128]{2,1,0:T(8,128)(2,1)S(1)}, u32[]{:S(2)}, u32[]{:S(2)}) collective-permute-start(bf16[32,32,128]{2,1,0:T(8,128)(2,1)S(1)} %get-tuple-element.22), channel_id=1, source_target_pairs={{0,1},{1,0},{2,3},{3,2},{4,5},{5,4},{6,7},{7,6},{8,9},{9,8},{10,11... | collective-permute-start | bytes 786440 | tf_op jit(solution)/shard_map/ppermute | solution.py:32
  17.9 7.4 %collective-permute-start.3 = (bf16[32,32,128]{2,1,0:T(8,128)(2,1)S(1)}, bf16[32,32,128]{2,1,0:T(8,128)(2,1)S(1)}, u32[]{:S(2)}, u32[]{:S(2)}) collective-permute-start(bf16[32,32,128]{2,1,0:T(8,128)(2,1)S(1)} %get-tuple-element.23), channel_id=1, source_target_pairs={{0,31},{1,2},{2,1},{3,4},{4,3},{5,6},{6,5},{7,8},{8,7},{9,10},{10,... | collective-permute-start | bytes 786440 | tf_op jit(solution)/shard_map/ppermute | solution.py:32
  25.3 0.0 collective-permute-start
  25.3 0.9 %collective-permute-start.1 = (bf16[32,32,128]{2,1,0:T(8,128)(2,1)S(1)}, bf16[32,32,128]{2,1,0:T(8,128)(2,1)S(1)}, u32[]{:S(2)}, u32[]{:S(2)}) collective-permute-start(bf16[32,32,128]{2,1,0:T(8,128)(2,1)S(1)} %get-tuple-element.21.m1_ref), channel_id=1, source_target_pairs={{0,31},{1,2},{2,1},{3,4},{4,3},{5,6},{6,5},{7,8},{8,7},{9,10},{10,... | collective-permute-start | bytes 786440 | tf_op jit(solution)/shard_map/ppermute | solution.py:32
  26.2 0.0 copy-done
  26.2 0.0 copy-done.1
  26.2 0.0 copy-done.3
  26.2 0.0 copy-done.4
  26.2 0.0 copy-done.5
  26.2 0.0 copy-done.6
  26.2 0.8 %matrix_weights.1 = (bf16[3584,256]{1,0:T(8,128)(2,1)S(1)}, bf16[4480,256]{1,0:T(8,128)(2,1)S(1)}, f32[8,256]{1,0:T(8,128)S(1)}) custom-call(bf16[49,32,64]{2,1,0:T(8,128)(2,1)S(1)} %bitcast.19, bf16[49,64,128]{2,1,0:T(8,128)(2,1)S(1)} %bitcast.18, f32[1,64]{1,0:T(1,128)S(1)} %bitcast.21, f32[1,64]{1,0:T(1,128)S(1)} %bitcast.22, f32[1,128]{1,0:T(1,128)S(1)} %bitcast.23, ...), custom_call_target="tpu_custom_call" | custom-call | bytes 8388608 | tf_op jit(solution)/shard_map/matrix_weights/pallas_call | solution.py:264
  27.1 0.0 collective-permute-done.2.ri0_ref
  27.1 3.9 %collective-permute-done.3.ri1_ref = bf16[32,32,128]{2,1,0:T(8,128)(2,1)S(1)} collective-permute-done((bf16[32,32,128]{2,1,0:T(8,128)(2,1)S(1)}, bf16[32,32,128]{2,1,0:T(8,128)(2,1)S(1)}, u32[]{:S(2)}, u32[]{:S(2)}) %collective-permute-start.3) | collective-permute-done | bytes 262176 | tf_op jit(solution)/shard_map/ppermute | solution.py:32
  30.9 0.9 %collective-permute-done.rb0_ref = bf16[32,32,128]{2,1,0:T(8,128)(2,1)S(1)} collective-permute-done((bf16[32,32,128]{2,1,0:T(8,128)(2,1)S(1)}, bf16[32,32,128]{2,1,0:T(8,128)(2,1)S(1)}, u32[]{:S(2)}, u32[]{:S(2)}) %collective-permute-start) | collective-permute-done | bytes 262176 | tf_op jit(solution)/shard_map/ppermute | solution.py:32
  31.9 5.7 %collective-permute-done.1.rb1_ref = bf16[32,32,128]{2,1,0:T(8,128)(2,1)S(1)} collective-permute-done((bf16[32,32,128]{2,1,0:T(8,128)(2,1)S(1)}, bf16[32,32,128]{2,1,0:T(8,128)(2,1)S(1)}, u32[]{:S(2)}, u32[]{:S(2)}) %collective-permute-start.1) | collective-permute-done | bytes 262176 | tf_op jit(solution)/shard_map/ppermute | solution.py:32
  37.6 4.9 %build_field.1 = (bf16[4,132,2,16,128]{4,3,2,1,0:T(8,128)(2,1)S(1)}, f32[7,272,128]{2,1,0:T(8,128)S(1)}, bf16[5,5,2,16,128]{4,3,2,1,0:T(8,128)(2,1)S(1)}, bf16[5,5,2,16,128]{4,3,2,1,0:T(8,128)(2,1)S(1)}) custom-call(f32[257,32,128]{2,1,0:T(8,128)S(1)} %get-tuple-element.19.acc, bf16[32,32,128]{2,1,0:T(8,128)(2,1)S(1)} %collective-permute-done.rb0_ref, ...), custom_call_target="tpu_custom_call" | custom-call | tf_op jit(solution)/shard_map/build_field/pallas_call | solution.py:361
  42.5 2.8 %collective-permute-start.4 = (bf16[5,5,2,16,128]{4,3,2,1,0:T(8,128)(2,1)S(1)}, bf16[5,5,2,16,128]{4,3,2,1,0:T(8,128)(2,1)S(1)}, u32[]{:S(2)}, u32[]{:S(2)}) collective-permute-start(bf16[5,5,2,16,128]{4,3,2,1,0:T(8,128)(2,1)S(1)} %get-tuple-element.28.ma_ref), channel_id=1, source_target_pairs={{0,16},{1,17},{2,18},{3,19},{4,20},{5,21},{6,22},{7,23},{8,24},{9,... | collective-permute-start | bytes 614408 | tf_op jit(solution)/shard_map/ppermute | solution.py:32
  45.2 0.0 collective-permute-start.5
  45.2 6.3 %first_conv.1.h_ref = bf16[5,64,2,16,128]{4,3,2,1,0:T(8,128)(2,1)S(1)} custom-call(bf16[4,132,2,16,128]{4,3,2,1,0:T(8,128)(2,1)S(1)} %get-tuple-element.24.f_ref, f32[7,272,128]{2,1,0:T(8,128)S(1)} %get-tuple-element.25.e_ref, bf16[3584,256]{1,0:T(8,128)(2,1)S(1)} %get-tuple-element.26.w_ref.w1_ref, f32[8,256]{1,0:T(8,128)S(1)} %get-tuple-element.27.v_ref), custom_call_target="tpu_custom_call" | custom-call | flops 4227858432 | bytes 12582912 | tf_op jit(solution)/shard_map/first_conv/pallas_call | solution.py:448
  51.5 0.0 collective-permute-done.4.ra_ref
  51.5 0.0 collective-permute-done.5.rb_ref
  51.5 5.1 %second_conv.1 = bf16[64,32,128]{2,1,0:T(8,128)(2,1)} custom-call(bf16[5,64,2,16,128]{4,3,2,1,0:T(8,128)(2,1)S(1)} %first_conv.1.h_ref, bf16[5,5,2,16,128]{4,3,2,1,0:T(8,128)(2,1)S(1)} %get-tuple-element.28.ma_ref, bf16[5,5,2,16,128]{4,3,2,1,0:T(8,128)(2,1)S(1)} %get-tuple-element.29.mb_ref, bf16[5,5,2,16,128]{4,3,2,1,0:T(8,128)(2,1)S(1)} %collective-permute-done.4.ra_ref, ...), custom_call_target="tpu_custom_call" | custom-call | tf_op jit(solution)/shard_map/second_conv/pallas_call | solution.py:588
Async XLA Ops:
  0.0 4.8 %copy-start.2 = (s32[1,1,512]{2,1,0:T(1,128)S(1)}, s32[1,1,512]{2,1,0:T(1,128)}, u32[]{:S(2)}) copy-start(s32[1,1,512]{2,1,0:T(1,128)} %param.15) | copy-start | bytes 6148
  0.7 0.7 %copy-start.7 = (s32[1,1,128]{2,1,0:T(1,128)S(1)}, s32[1,1,128]{2,1,0:T(1,128)}, u32[]{:S(2)}) copy-start(s32[1,1,128]{2,1,0:T(1,128)} %param.19) | copy-start | bytes 1540
  4.8 21.4 %copy-start = (bf16[7,7,64,128]{3,2,1,0:T(8,128)(2,1)S(1)}, bf16[7,7,64,128]{3,2,1,0:T(8,128)(2,1)}, u32[]{:S(2)}) copy-start(bf16[7,7,64,128]{3,2,1,0:T(8,128)(2,1)} %param.23) | copy-start | bytes 2408452
  4.8 21.4 %copy-start.1 = (bf16[7,7,32,64]{3,2,1,0:T(8,128)(2,1)S(1)}, bf16[7,7,32,64]{3,2,1,0:T(8,128)(2,1)}, u32[]{:S(2)}) copy-start(bf16[7,7,32,64]{3,2,1,0:T(8,128)(2,1)} %param.20) | copy-start | bytes 602116
  4.9 21.4 %copy-start.3 = (f32[64]{0:T(128)S(1)}, f32[64]{0:T(128)}, u32[]{:S(2)}) copy-start(f32[64]{0:T(128)} %param.21) | copy-start | bytes 772
  4.9 21.3 %copy-start.4 = (f32[64]{0:T(128)S(1)}, f32[64]{0:T(128)}, u32[]{:S(2)}) copy-start(f32[64]{0:T(128)} %param.22) | copy-start | bytes 772
  4.9 21.3 %copy-start.5 = (f32[128]{0:T(128)S(1)}, f32[128]{0:T(128)}, u32[]{:S(2)}) copy-start(f32[128]{0:T(128)} %param.24) | copy-start | bytes 1540
  4.9 21.3 %copy-start.6 = (f32[128]{0:T(128)S(1)}, f32[128]{0:T(128)}, u32[]{:S(2)}) copy-start(f32[128]{0:T(128)} %param.25) | copy-start | bytes 1540
  15.7 11.4 %collective-permute-start.2 = (bf16[32,32,128]{2,1,0:T(8,128)(2,1)S(1)}, bf16[32,32,128]{2,1,0:T(8,128)(2,1)S(1)}, u32[]{:S(2)}, u32[]{:S(2)}) collective-permute-start(bf16[32,32,128]{2,1,0:T(8,128)(2,1)S(1)} %get-tuple-element.22), channel_id=1, source_target_pairs={{0,1},{1,0},{2,3},{3,2},{4,5},{5,4},{6,7},{7,6},{8,9},{9,8},{10,11... | collective-permute-start | bytes 786440 | tf_op jit(solution)/shard_map/ppermute | solution.py:32
  17.9 13.1 %collective-permute-start.3 = (bf16[32,32,128]{2,1,0:T(8,128)(2,1)S(1)}, bf16[32,32,128]{2,1,0:T(8,128)(2,1)S(1)}, u32[]{:S(2)}, u32[]{:S(2)}) collective-permute-start(bf16[32,32,128]{2,1,0:T(8,128)(2,1)S(1)} %get-tuple-element.23), channel_id=1, source_target_pairs={{0,31},{1,2},{2,1},{3,4},{4,3},{5,6},{6,5},{7,8},{8,7},{9,10},{10,... | collective-permute-start | bytes 786440 | tf_op jit(solution)/shard_map/ppermute | solution.py:32
  25.3 6.6 %collective-permute-start = (bf16[32,32,128]{2,1,0:T(8,128)(2,1)S(1)}, bf16[32,32,128]{2,1,0:T(8,128)(2,1)S(1)}, u32[]{:S(2)}, u32[]{:S(2)}) collective-permute-start(bf16[32,32,128]{2,1,0:T(8,128)(2,1)S(1)} %get-tuple-element.20.m0_ref), channel_id=1, source_target_pairs={{0,1},{1,0},{2,3},{3,2},{4,5},{5,4},{6,7},{7,6},{8,9},{9,8},{10,11... | collective-permute-start | bytes 786440 | tf_op jit(solution)/shard_map/ppermute | solution.py:32
  25.3 12.3 %collective-permute-start.1 = (bf16[32,32,128]{2,1,0:T(8,128)(2,1)S(1)}, bf16[32,32,128]{2,1,0:T(8,128)(2,1)S(1)}, u32[]{:S(2)}, u32[]{:S(2)}) collective-permute-start(bf16[32,32,128]{2,1,0:T(8,128)(2,1)S(1)} %get-tuple-element.21.m1_ref), channel_id=1, source_target_pairs={{0,31},{1,2},{2,1},{3,4},{4,3},{5,6},{6,5},{7,8},{8,7},{9,10},{10,... | collective-permute-start | bytes 786440 | tf_op jit(solution)/shard_map/ppermute | solution.py:32
  42.5 9.1 %collective-permute-start.4 = (bf16[5,5,2,16,128]{4,3,2,1,0:T(8,128)(2,1)S(1)}, bf16[5,5,2,16,128]{4,3,2,1,0:T(8,128)(2,1)S(1)}, u32[]{:S(2)}, u32[]{:S(2)}) collective-permute-start(bf16[5,5,2,16,128]{4,3,2,1,0:T(8,128)(2,1)S(1)} %get-tuple-element.28.ma_ref), channel_id=1, source_target_pairs={{0,16},{1,17},{2,18},{3,19},{4,20},{5,21},{6,22},{7,23},{8,24},{9,... | collective-permute-start | bytes 614408 | tf_op jit(solution)/shard_map/ppermute | solution.py:32
  45.2 6.3 %collective-permute-start.5 = (bf16[5,5,2,16,128]{4,3,2,1,0:T(8,128)(2,1)S(1)}, bf16[5,5,2,16,128]{4,3,2,1,0:T(8,128)(2,1)S(1)}, u32[]{:S(2)}, u32[]{:S(2)}) collective-permute-start(bf16[5,5,2,16,128]{4,3,2,1,0:T(8,128)(2,1)S(1)} %get-tuple-element.29.mb_ref), channel_id=1, source_target_pairs={{0,32},{1,33},{2,34},{3,35},{4,36},{5,37},{6,38},{7,39},{8,40},{9,... | collective-permute-start | bytes 614408 | tf_op jit(solution)/shard_map/ppermute | solution.py:32

commit v3 on v2

--- a/solution.py
+++ b/solution.py
@@ -91,9 +91,13 @@
         fill(m1_ref, m0_ref)
 
 
-def border_kernel(btarget, x_hbm, w_hbm, m0_ref, m1_ref, token, xv, wv, st, sb, acc, sem):
+def border_kernel(
+    btarget_hbm, x_hbm, w_hbm, m0_ref, m1_ref, token, xv, wv, st, sb, acc, btarget, sem
+):
     states = pltpu.make_async_copy(x_hbm, xv, sem.at[4])
     states.start()
+    targets = pltpu.make_async_copy(btarget_hbm, btarget, sem.at[5])
+    targets.start()
     chunks = [
         pltpu.make_async_copy(
             w_hbm.at[pl.ds(32 * c, 32)], wv.at[pl.ds(32 * c, 32)], sem.at[c]
@@ -113,6 +117,7 @@
         st[pl.ds(c + 1, 128, stride=16), :] = out[:, 128:]
     for q in range(8):
         sb[16 * q : 16 * q + 16] = st[256 * q : 256 * q + 256].astype(BF16).reshape(16, 16, 128)
+    targets.wait()
     for c in range(4):
         chunks[c].wait()
 
@@ -141,7 +146,7 @@
     return pl.pallas_call(
         border_kernel,
         name="border_sums",
-        in_specs=[SMEM, HBM, HBM],
+        in_specs=[HBM, HBM, HBM],
         out_specs=[VMEM, VMEM, VMEM],
         out_shape=[side, side, jax.ShapeDtypeStruct((8, 128), F32)],
         scratch_shapes=[
@@ -150,13 +155,14 @@
             pltpu.VMEM((2048, 128), F32),
             pltpu.VMEM((128, 16, 128), BF16),
             pltpu.VMEM((64, 32, 128), F32),
-            pltpu.SemaphoreType.DMA((5,)),
+            pltpu.SMEM((128,), jnp.int32),
+            pltpu.SemaphoreType.DMA((6,)),
         ],
         cost_estimate=pl.CostEstimate(
             flops=2 * 128 * 32 * 64 * 128, bytes_accessed=4 << 20, transcendentals=0
         ),
         compiler_params=pltpu.CompilerParams(vmem_limit_bytes=BIG),
-    )(btarget, in_hbm(jnp.transpose(bstate, (1, 2, 0))), in_hbm(bweight))
+    )(in_hbm(btarget), in_hbm(jnp.transpose(bstate, (1, 2, 0))), in_hbm(bweight))
 
 
 def sums_kernel(
@@ -274,11 +280,7 @@
     )(k1.reshape(49, 32, 64), k2.reshape(49, 64, 128), b1[None], g1[None], b2[None], g2[None])
 
 
-def field_kernel(
-    acc, rb0_ref, rb1_ref, ri0_ref, ri1_ref, m0_ref, m1_ref, f_ref, e_ref, ma_ref, mb_ref, fs, et
-):
-    odd = lax.axis_index("lon") % 2
-    upper = lax.axis_index("lat") % 2
+def selectors():
     rows = lax.broadcasted_iota(jnp.int32, (32, 128), 0)
     pix = lax.broadcasted_iota(jnp.int32, (32, 128), 1)
     pick = (pix // 4 == (rows % 8) * 4 + rows // 8).astype(F32).astype(BF16)
@@ -286,47 +288,93 @@
         lax.broadcasted_iota(jnp.int32, (128, 128), 0) // 32
         == lax.broadcasted_iota(jnp.int32, (128, 128), 1) % 4
     ).astype(F32).astype(BF16)
+    return pick, keep
+
+
+def place_pair(pair, pc0, y, fs, pick, keep, edge):
+    spread = jnp.concatenate(
+        [jnp.concatenate([v.astype(BF16)] * 4, axis=0) * keep for v in pair], axis=0
+    )
+    both = nt_dot(pick, spread)
+    for h in range(2):
+        pc = pc0 + h
+        for k in range(4):
+            v = both[8 * k : 8 * k + 8, 128 * h : 128 * h + 128]
+            g = 2 * pc + k // 2
+            kk = 4 * pc + k
+            if 0 <= pc < 8:
+                fs[y, k % 2, pl.ds(g, 8, stride=16), :] = v
+            if k % 2 == 0 and 1 <= g <= 16:
+                fs[y, 3, pl.ds(g - 1, 8, stride=16), :] = v
+            if k % 2 == 1 and -1 <= g <= 14:
+                fs[y, 2, pl.ds(g + 1, 8, stride=16), :] = v
+            if kk in (-3, -2, -1, 0, 31, 32, 33):
+                edge(kk + 3 if kk <= 0 else kk - 27, v)
+
+
+def interior_kernel(acc, f_ref, fs):
+    pick, keep = selectors()
     f_ref[:, 0:2] = jnp.zeros((4, 2, 2, 16, 128), BF16)
     f_ref[:, 130:132] = jnp.zeros((4, 2, 2, 16, 128), BF16)
-    et[...] = jnp.zeros_like(et)
-    is_odd = odd == 1
+    fs[...] = jnp.zeros_like(fs)
 
     def step(i, carry):
         for y in range(4):
-            east_border = jnp.where(is_odd, rb1_ref[4 * i + y], rb0_ref[4 * i + y]).astype(F32)
-            east_inner = jnp.where(is_odd, ri1_ref[4 * i + y], ri0_ref[4 * i + y]).astype(F32)
-            west_border = jnp.where(is_odd, rb0_ref[4 * i + y], rb1_ref[4 * i + y]).astype(F32)
-            west_inner = jnp.where(is_odd, ri0_ref[4 * i + y], ri1_ref[4 * i + y]).astype(F32)
-            own_east = jnp.where(is_odd, m1_ref[4 * i + y], m0_ref[4 * i + y]).astype(F32)
-            own_west = jnp.where(is_odd, m0_ref[4 * i + y], m1_ref[4 * i + y]).astype(F32)
-            patches = [acc[32 * i + 8 * y + c] for c in range(8)]
-            patches[0] = patches[0] + west_border
-            patches[7] = patches[7] + east_border
-            patches = [west_inner + own_west] + patches + [east_inner + own_east]
-            for c in range(0, 10, 2):
-                pair = [patches[c].astype(BF16), patches[c + 1].astype(BF16)]
-                spread = jnp.concatenate(
-                    [jnp.concatenate([v] * 4, axis=0) * keep for v in pair], axis=0
-                )
-                both = nt_dot(pick, spread)
-                for h in range(2):
-                    pc = c + h - 1
-                    for k in range(4):
-                        v = both[8 * k : 8 * k + 8, 128 * h : 128 * h + 128]
-                        g = 2 * pc + k // 2
-                        kk = 4 * pc + k
-                        if 0 <= pc < 8:
-                            fs[y, k % 2, pl.ds(g, 8, stride=16), :] = v
-                        if k % 2 == 0 and 1 <= g <= 16:
-                            fs[y, 3, pl.ds(g - 1, 8, stride=16), :] = v
-                        if k % 2 == 1 and -1 <= g <= 14:
-                            fs[y, 2, pl.ds(g + 1, 8, stride=16), :] = v
-                        if kk in (-3, -2, -1, 0, 31, 32, 33):
-                            slot = kk + 3 if kk <= 0 else kk - 27
-                            e_ref[slot, pl.ds(8 + 32 * i + 8 * y, 8), :] = v
-                            et[y, pl.ds(slot, 8, stride=16), :] = v
+            for c in range(1, 7, 2):
+                pair = [acc[32 * i + 8 * y + c], acc[32 * i + 8 * y + c + 1]]
+                place_pair(pair, c, y, fs, pick, keep, None)
             for a in range(4):
                 f_ref[a, pl.ds(2 + 16 * i + 4 * y, 4)] = fs[y, a].astype(BF16).reshape(4, 2, 16, 128)
+        return carry
+
+    lax.fori_loop(0, 8, step, 0)
+
+
+def build_interior(acc):
+    return pl.pallas_call(
+        interior_kernel,
+        name="build_interior",
+        in_specs=[VMEM],
+        out_specs=VMEM,
+        out_shape=pltpu.VMEM((4, 132, 2, 16, 128), BF16),
+        scratch_shapes=[pltpu.VMEM((4, 4, 128, 128), F32)],
+        cost_estimate=pl.CostEstimate(flops=1 << 28, bytes_accessed=8 << 20, transcendentals=0),
+        compiler_params=pltpu.CompilerParams(vmem_limit_bytes=16 << 20),
+    )(acc)
+
+
+def field_kernel(
+    inside, acc, rb0_ref, rb1_ref, ri0_ref, ri1_ref, m0_ref, m1_ref,
+    f_ref, e_ref, ma_ref, mb_ref, fs, et,
+):
+    odd = lax.axis_index("lon") % 2
+    upper = lax.axis_index("lat") % 2
+    pick, keep = selectors()
+    et[...] = jnp.zeros_like(et)
+    fs[...] = jnp.zeros_like(fs)
+    is_odd = odd == 1
+
+    def step(i, carry):
+        for y in range(4):
+            n = 4 * i + y
+            east_border = jnp.where(is_odd, rb1_ref[n], rb0_ref[n]).astype(F32)
+            east_inner = jnp.where(is_odd, ri1_ref[n], ri0_ref[n]).astype(F32)
+            west_border = jnp.where(is_odd, rb0_ref[n], rb1_ref[n]).astype(F32)
+            west_inner = jnp.where(is_odd, ri0_ref[n], ri1_ref[n]).astype(F32)
+            own_east = jnp.where(is_odd, m1_ref[n], m0_ref[n]).astype(F32)
+            own_west = jnp.where(is_odd, m0_ref[n], m1_ref[n]).astype(F32)
+
+            def edge(slot, v, y=y):
+                e_ref[slot, pl.ds(8 + 32 * i + 8 * y, 8), :] = v
+                et[y, pl.ds(slot, 8, stride=16), :] = v
+
+            west = [west_inner + own_west, acc[8 * n] + west_border]
+            east = [acc[8 * n + 7] + east_border, east_inner + own_east]
+            place_pair(west, -1, y, fs, pick, keep, edge)
+            place_pair(east, 7, y, fs, pick, keep, edge)
+            for a in range(4):
+                to = pl.ds(2 + 16 * i + 4 * y, 4)
+                f_ref[a, to] = inside[a, to] + fs[y, a].astype(BF16).reshape(4, 2, 16, 128)
 
         def send(ref, first, start):
             for a in range(4):
@@ -356,12 +404,12 @@
     lax.fori_loop(0, 8, step, 0)
 
 
-def build_field(acc, *sides):
+def build_field(inside, acc, *sides):
     msg = jax.ShapeDtypeStruct((5, 5, 2, 16, 128), BF16)
     return pl.pallas_call(
         field_kernel,
         name="build_field",
-        in_specs=[VMEM] * 7,
+        in_specs=[VMEM] * 8,
         out_specs=[VMEM] * 4,
         out_shape=[
             pltpu.VMEM((4, 132, 2, 16, 128), BF16),
@@ -369,12 +417,13 @@
             msg,
             msg,
         ],
+        input_output_aliases={0: 0},
         scratch_shapes=[
             pltpu.VMEM((4, 4, 128, 128), F32),
             pltpu.VMEM((4, 128, 128), F32),
         ],
-        compiler_params=pltpu.CompilerParams(vmem_limit_bytes=24 << 20),
-    )(acc, *sides)
+        compiler_params=pltpu.CompilerParams(vmem_limit_bytes=16 << 20),
+    )(inside, acc, *sides)
 
 
 ORDER = (2, 0, 1, 3)
@@ -630,7 +679,8 @@
     ri0 = exchange(i0, LON_EVEN)
     ri1 = exchange(i1, LON_ODD)
     w1, w2, vec = matrix_weights(kernel_one, kernel_two, bias_one, gain_one, bias_two, gain_two)
-    f, e, ma, mb = build_field(acc, rb0, rb1, ri0, ri1, m0, m1)
+    inside = build_interior(acc)
+    f, e, ma, mb = build_field(inside, acc, rb0, rb1, ri0, ri1, m0, m1)
     ra = exchange(ma, LAT_OUTER)
     rb = exchange(mb, LAT_INNER)
     h = first_conv(f, e, w1, vec)

time: 56.8 us -> 54.1 us (0.952)
  waiting for transfers between devices: 10.5 us -> 6.61 us
  Pallas kernels: 31.4 us -> 33.2 us
  local copies, waits for them, and re-layouts: 0.69 us -> 0.04 us
    ppermute x6, waiting for transfers between devices: 10.5 us -> 6.61 us  [exchange(): return lax.ppermute(block, ('lat', 'lon'), pairs)]
    pallas_call x2 -> x3, Pallas kernels: 8.34 us -> 10.2 us  [the longest x1 3.85 us: build_interior(): pl.pallas_call(interior_kernel, name='build_interior', in_specs=[VMEM], o...]
    unnamed x16 -> x14, local copies, waits for them, and re-layouts: 0.69 us -> 0.04 us
  transfers between devices with their start and end apart: 6 -> 6, of which waited for: 3 -> 2; matrix products, arithmetic and copies ran while one was open for 0% -> 0% of each run, Pallas kernels for 13% -> 20%
where the time goes in v3:
time: 54.1 us; the launch traced here: 53.9 us
  Pallas kernels  33.2 us (61%)
  starting transfers between devices  13.3 us (25%)
  waiting for transfers between devices  6.61 us (12%)
  between operations  0.82 us (2%)
    ppermute x6, starting transfers between devices, exchange(): return lax.ppermute(block, ('lat', 'lon'), pairs)  13.3 us
    pallas_call x1, Pallas kernels, inner_sums(): pl.pallas_call(sums_kernel, name='inner_sums', in_specs=[SMEM, SMEM, VMEM...  10.8 us
    ppermute x6, waiting for transfers between devices, exchange(): return lax.ppermute(block, ('lat', 'lon'), pairs)  6.61 us
    pallas_call x1, Pallas kernels, first_conv(): pl.pallas_call(first_kernel, name='first_conv', in_specs=[VMEM] * 4, out_...  6.29 us
    pallas_call x1, Pallas kernels, second_conv(): pl.pallas_call(second_kernel, name='second_conv', in_specs=[VMEM] * 8, ou...  5.03 us
    pallas_call x1, Pallas kernels, build_interior(): pl.pallas_call(interior_kernel, name='build_interior', in_specs=[VMEM], o...  3.85 us
    pallas_call x1, Pallas kernels, build_field(): pl.pallas_call(field_kernel, name='build_field', in_specs=[VMEM] * 8, out...  3.39 us
    pallas_call x1, Pallas kernels, border_sums(): pl.pallas_call(border_kernel, name='border_sums', in_specs=[HBM, HBM, HBM...  2.96 us
  transfers between devices with their start and end apart: 6, of which 2 were waited for; matrix products, arithmetic and copies ran while one was open for 0% of the time, Pallas kernels for 20%

profile of v3, /device:TPU:1, one launch (start us, length us, event | category | flops | bytes accessed | tf_op | source)
XLA Modules:
  0.0 53.9 jit_solution(14190272365014859203)
XLA Ops:
  0.0 0.0 copy-start.2
  0.7 3.0 %border_sums.1 = (bf16[32,32,128]{2,1,0:T(8,128)(2,1)S(1)}, bf16[32,32,128]{2,1,0:T(8,128)(2,1)S(1)}, f32[8,128]{1,0:T(8,128)S(1)}) custom-call(s32[128]{0:T(128)} %bitcast.29, bf16[32,64,128]{2,1,0:T(8,128)(2,1)} %bitcast.28, bf16[128,64,128]{2,1,0:T(8,128)(2,1)} %bitcast.26), custom_call_target="tpu_custom_call" | custom-call | flops 67108864 | bytes 4194304 | tf_op jit(solution)/shard_map/border_sums/pallas_call | solution.py:146
  3.6 0.0 copy-done.2
  3.6 0.0 copy-start
  3.7 0.0 copy-start.1
  3.7 0.0 copy-start.3
  3.7 0.0 copy-start.4
  3.7 0.0 copy-start.5
  3.7 0.0 copy-start.6
  3.7 10.8 %inner_sums.1 = (f32[257,32,128]{2,1,0:T(8,128)S(1)}, bf16[32,32,128]{2,1,0:T(8,128)(2,1)S(1)}, bf16[32,32,128]{2,1,0:T(8,128)(2,1)S(1)}) custom-call(s32[512]{0:T(512)S(1)} %bitcast.20, s32[1]{0:T(128)} %bitcast.17.count, f32[8,128]{1,0:T(8,128)S(1)} %get-tuple-element.18.after, bf16[32,64,512]{2,1,0:T(8,128)(2,1)} %bitcast.27, bf16[512,64,128]{2,1,0:T(8,128)(2,1)} %bitcast.25), custom_call_target="tpu_custom_call" | custom-call | flops 268435456 | bytes 16777216 | tf_op jit(solution)/shard_map/inner_sums/pallas_call | solution.py:229
  14.5 2.2 %collective-permute-start.2 = (bf16[32,32,128]{2,1,0:T(8,128)(2,1)S(1)}, bf16[32,32,128]{2,1,0:T(8,128)(2,1)S(1)}, u32[]{:S(2)}, u32[]{:S(2)}) collective-permute-start(bf16[32,32,128]{2,1,0:T(8,128)(2,1)S(1)} %get-tuple-element.22), channel_id=1, source_target_pairs={{0,1},{1,0},{2,3},{3,2},{4,5},{5,4},{6,7},{7,6},{8,9},{9,8},{10,11... | collective-permute-start | bytes 786440 | tf_op jit(solution)/shard_map/ppermute | solution.py:32
  16.7 7.4 %collective-permute-start.3 = (bf16[32,32,128]{2,1,0:T(8,128)(2,1)S(1)}, bf16[32,32,128]{2,1,0:T(8,128)(2,1)S(1)}, u32[]{:S(2)}, u32[]{:S(2)}) collective-permute-start(bf16[32,32,128]{2,1,0:T(8,128)(2,1)S(1)} %get-tuple-element.23), channel_id=1, source_target_pairs={{0,31},{1,2},{2,1},{3,4},{4,3},{5,6},{6,5},{7,8},{8,7},{9,10},{10,... | collective-permute-start | bytes 786440 | tf_op jit(solution)/shard_map/ppermute | solution.py:32
  24.1 0.0 collective-permute-start
  24.1 0.9 %collective-permute-start.1 = (bf16[32,32,128]{2,1,0:T(8,128)(2,1)S(1)}, bf16[32,32,128]{2,1,0:T(8,128)(2,1)S(1)}, u32[]{:S(2)}, u32[]{:S(2)}) collective-permute-start(bf16[32,32,128]{2,1,0:T(8,128)(2,1)S(1)} %get-tuple-element.21.m1_ref), channel_id=1, source_target_pairs={{0,31},{1,2},{2,1},{3,4},{4,3},{5,6},{6,5},{7,8},{8,7},{9,10},{10,... | collective-permute-start | bytes 786440 | tf_op jit(solution)/shard_map/ppermute | solution.py:32
  25.0 0.0 copy-done
  25.0 0.0 copy-done.1
  25.0 0.0 copy-done.3
  25.0 0.0 copy-done.4
  25.0 0.0 copy-done.5
  25.1 0.0 copy-done.6
  25.1 0.8 %matrix_weights.1 = (bf16[3584,256]{1,0:T(8,128)(2,1)S(1)}, bf16[4480,256]{1,0:T(8,128)(2,1)S(1)}, f32[8,256]{1,0:T(8,128)S(1)}) custom-call(bf16[49,32,64]{2,1,0:T(8,128)(2,1)S(1)} %bitcast.19, bf16[49,64,128]{2,1,0:T(8,128)(2,1)S(1)} %bitcast.18, f32[1,64]{1,0:T(1,128)S(1)} %bitcast.21, f32[1,64]{1,0:T(1,128)S(1)} %bitcast.22, f32[1,128]{1,0:T(1,128)S(1)} %bitcast.23, ...), custom_call_target="tpu_custom_call" | custom-call | bytes 8388608 | tf_op jit(solution)/shard_map/matrix_weights/pallas_call | solution.py:270
  25.9 3.9 %build_interior.1.inside = bf16[4,132,2,16,128]{4,3,2,1,0:T(8,128)(2,1)S(1)} custom-call(f32[257,32,128]{2,1,0:T(8,128)S(1)} %get-tuple-element.19.acc), custom_call_target="tpu_custom_call" | custom-call | flops 268435456 | bytes 8388608 | tf_op jit(solution)/shard_map/build_interior/pallas_call | solution.py:334
  29.8 0.0 collective-permute-done.2.ri0_ref
  29.8 0.0 collective-permute-done.3.ri1_ref
  29.8 0.9 %collective-permute-done.rb0_ref = bf16[32,32,128]{2,1,0:T(8,128)(2,1)S(1)} collective-permute-done((bf16[32,32,128]{2,1,0:T(8,128)(2,1)S(1)}, bf16[32,32,128]{2,1,0:T(8,128)(2,1)S(1)}, u32[]{:S(2)}, u32[]{:S(2)}) %collective-permute-start) | collective-permute-done | bytes 262176 | tf_op jit(solution)/shard_map/ppermute | solution.py:32
  30.7 5.7 %collective-permute-done.1.rb1_ref = bf16[32,32,128]{2,1,0:T(8,128)(2,1)S(1)} collective-permute-done((bf16[32,32,128]{2,1,0:T(8,128)(2,1)S(1)}, bf16[32,32,128]{2,1,0:T(8,128)(2,1)S(1)}, u32[]{:S(2)}, u32[]{:S(2)}) %collective-permute-start.1) | collective-permute-done | bytes 262176 | tf_op jit(solution)/shard_map/ppermute | solution.py:32
  36.4 3.4 %build_field.1 = (bf16[4,132,2,16,128]{4,3,2,1,0:T(8,128)(2,1)S(1)}, f32[7,272,128]{2,1,0:T(8,128)S(1)}, bf16[5,5,2,16,128]{4,3,2,1,0:T(8,128)(2,1)S(1)}, bf16[5,5,2,16,128]{4,3,2,1,0:T(8,128)(2,1)S(1)}) custom-call(bf16[4,132,2,16,128]{4,3,2,1,0:T(8,128)(2,1)S(1)} %build_interior.1.inside, ...), custom_call_target="tpu_custom_call", output_to_operand_aliasing={{0}: (0, {})} | custom-call | tf_op jit(solution)/shard_map/build_field/pallas_call | solution.py:409
  39.8 2.8 %collective-permute-start.4 = (bf16[5,5,2,16,128]{4,3,2,1,0:T(8,128)(2,1)S(1)}, bf16[5,5,2,16,128]{4,3,2,1,0:T(8,128)(2,1)S(1)}, u32[]{:S(2)}, u32[]{:S(2)}) collective-permute-start(bf16[5,5,2,16,128]{4,3,2,1,0:T(8,128)(2,1)S(1)} %get-tuple-element.28.ma_ref), channel_id=1, source_target_pairs={{0,16},{1,17},{2,18},{3,19},{4,20},{5,21},{6,22},{7,23},{8,24},{9,... | collective-permute-start | bytes 614408 | tf_op jit(solution)/shard_map/ppermute | solution.py:32
  42.6 0.0 collective-permute-start.5
  42.6 6.3 %first_conv.1.h_ref = bf16[5,64,2,16,128]{4,3,2,1,0:T(8,128)(2,1)S(1)} custom-call(bf16[4,132,2,16,128]{4,3,2,1,0:T(8,128)(2,1)S(1)} %get-tuple-element.24.f_ref, f32[7,272,128]{2,1,0:T(8,128)S(1)} %get-tuple-element.25.e_ref, bf16[3584,256]{1,0:T(8,128)(2,1)S(1)} %get-tuple-element.26.w_ref.w1_ref, f32[8,256]{1,0:T(8,128)S(1)} %get-tuple-element.27.v_ref), custom_call_target="tpu_custom_call" | custom-call | flops 4227858432 | bytes 12582912 | tf_op jit(solution)/shard_map/first_conv/pallas_call | solution.py:497
  48.9 0.0 collective-permute-done.4.ra_ref
  48.9 0.0 collective-permute-done.5.rb_ref
  48.9 5.0 %second_conv.1 = bf16[64,32,128]{2,1,0:T(8,128)(2,1)} custom-call(bf16[5,64,2,16,128]{4,3,2,1,0:T(8,128)(2,1)S(1)} %first_conv.1.h_ref, bf16[5,5,2,16,128]{4,3,2,1,0:T(8,128)(2,1)S(1)} %get-tuple-element.28.ma_ref, bf16[5,5,2,16,128]{4,3,2,1,0:T(8,128)(2,1)S(1)} %get-tuple-element.29.mb_ref, bf16[5,5,2,16,128]{4,3,2,1,0:T(8,128)(2,1)S(1)} %collective-permute-done.4.ra_ref, ...), custom_call_target="tpu_custom_call" | custom-call | tf_op jit(solution)/shard_map/second_conv/pallas_call | solution.py:637
Async XLA Ops:
  0.0 3.6 %copy-start.2 = (s32[1,1,512]{2,1,0:T(1,128)S(1)}, s32[1,1,512]{2,1,0:T(1,128)}, u32[]{:S(2)}) copy-start(s32[1,1,512]{2,1,0:T(1,128)} %param.15) | copy-start | bytes 6148
  3.6 21.4 %copy-start = (bf16[7,7,64,128]{3,2,1,0:T(8,128)(2,1)S(1)}, bf16[7,7,64,128]{3,2,1,0:T(8,128)(2,1)}, u32[]{:S(2)}) copy-start(bf16[7,7,64,128]{3,2,1,0:T(8,128)(2,1)} %param.23) | copy-start | bytes 2408452
  3.7 21.4 %copy-start.1 = (bf16[7,7,32,64]{3,2,1,0:T(8,128)(2,1)S(1)}, bf16[7,7,32,64]{3,2,1,0:T(8,128)(2,1)}, u32[]{:S(2)}) copy-start(bf16[7,7,32,64]{3,2,1,0:T(8,128)(2,1)} %param.20) | copy-start | bytes 602116
  3.7 21.4 %copy-start.3 = (f32[64]{0:T(128)S(1)}, f32[64]{0:T(128)}, u32[]{:S(2)}) copy-start(f32[64]{0:T(128)} %param.21) | copy-start | bytes 772
  3.7 21.4 %copy-start.4 = (f32[64]{0:T(128)S(1)}, f32[64]{0:T(128)}, u32[]{:S(2)}) copy-start(f32[64]{0:T(128)} %param.22) | copy-start | bytes 772
  3.7 21.3 %copy-start.5 = (f32[128]{0:T(128)S(1)}, f32[128]{0:T(128)}, u32[]{:S(2)}) copy-start(f32[128]{0:T(128)} %param.24) | copy-start | bytes 1540
  3.7 21.3 %copy-start.6 = (f32[128]{0:T(128)S(1)}, f32[128]{0:T(128)}, u32[]{:S(2)}) copy-start(f32[128]{0:T(128)} %param.25) | copy-start | bytes 1540
  14.5 15.3 %collective-permute-start.2 = (bf16[32,32,128]{2,1,0:T(8,128)(2,1)S(1)}, bf16[32,32,128]{2,1,0:T(8,128)(2,1)S(1)}, u32[]{:S(2)}, u32[]{:S(2)}) collective-permute-start(bf16[32,32,128]{2,1,0:T(8,128)(2,1)S(1)} %get-tuple-element.22), channel_id=1, source_target_pairs={{0,1},{1,0},{2,3},{3,2},{4,5},{5,4},{6,7},{7,6},{8,9},{9,8},{10,11... | collective-permute-start | bytes 786440 | tf_op jit(solution)/shard_map/ppermute | solution.py:32
  16.7 13.1 %collective-permute-start.3 = (bf16[32,32,128]{2,1,0:T(8,128)(2,1)S(1)}, bf16[32,32,128]{2,1,0:T(8,128)(2,1)S(1)}, u32[]{:S(2)}, u32[]{:S(2)}) collective-permute-start(bf16[32,32,128]{2,1,0:T(8,128)(2,1)S(1)} %get-tuple-element.23), channel_id=1, source_target_pairs={{0,31},{1,2},{2,1},{3,4},{4,3},{5,6},{6,5},{7,8},{8,7},{9,10},{10,... | collective-permute-start | bytes 786440 | tf_op jit(solution)/shard_map/ppermute | solution.py:32
  24.1 6.6 %collective-permute-start = (bf16[32,32,128]{2,1,0:T(8,128)(2,1)S(1)}, bf16[32,32,128]{2,1,0:T(8,128)(2,1)S(1)}, u32[]{:S(2)}, u32[]{:S(2)}) collective-permute-start(bf16[32,32,128]{2,1,0:T(8,128)(2,1)S(1)} %get-tuple-element.20.m0_ref), channel_id=1, source_target_pairs={{0,1},{1,0},{2,3},{3,2},{4,5},{5,4},{6,7},{7,6},{8,9},{9,8},{10,11... | collective-permute-start | bytes 786440 | tf_op jit(solution)/shard_map/ppermute | solution.py:32
  24.1 12.3 %collective-permute-start.1 = (bf16[32,32,128]{2,1,0:T(8,128)(2,1)S(1)}, bf16[32,32,128]{2,1,0:T(8,128)(2,1)S(1)}, u32[]{:S(2)}, u32[]{:S(2)}) collective-permute-start(bf16[32,32,128]{2,1,0:T(8,128)(2,1)S(1)} %get-tuple-element.21.m1_ref), channel_id=1, source_target_pairs={{0,31},{1,2},{2,1},{3,4},{4,3},{5,6},{6,5},{7,8},{8,7},{9,10},{10,... | collective-permute-start | bytes 786440 | tf_op jit(solution)/shard_map/ppermute | solution.py:32
  39.8 9.1 %collective-permute-start.4 = (bf16[5,5,2,16,128]{4,3,2,1,0:T(8,128)(2,1)S(1)}, bf16[5,5,2,16,128]{4,3,2,1,0:T(8,128)(2,1)S(1)}, u32[]{:S(2)}, u32[]{:S(2)}) collective-permute-start(bf16[5,5,2,16,128]{4,3,2,1,0:T(8,128)(2,1)S(1)} %get-tuple-element.28.ma_ref), channel_id=1, source_target_pairs={{0,16},{1,17},{2,18},{3,19},{4,20},{5,21},{6,22},{7,23},{8,24},{9,... | collective-permute-start | bytes 614408 | tf_op jit(solution)/shard_map/ppermute | solution.py:32
  42.6 6.3 %collective-permute-start.5 = (bf16[5,5,2,16,128]{4,3,2,1,0:T(8,128)(2,1)S(1)}, bf16[5,5,2,16,128]{4,3,2,1,0:T(8,128)(2,1)S(1)}, u32[]{:S(2)}, u32[]{:S(2)}) collective-permute-start(bf16[5,5,2,16,128]{4,3,2,1,0:T(8,128)(2,1)S(1)} %get-tuple-element.29.mb_ref), channel_id=1, source_target_pairs={{0,32},{1,33},{2,34},{3,35},{4,36},{5,37},{6,38},{7,39},{8,40},{9,... | collective-permute-start | bytes 614408 | tf_op jit(solution)/shard_map/ppermute | solution.py:32

commit v4 on v3

--- a/solution.py
+++ b/solution.py
@@ -166,7 +166,8 @@
 
 
 def sums_kernel(
-    target, count, after, x_hbm, w_hbm, acc_ref, m0_ref, m1_ref, xv, wv, st, sb, xsem, wsem
+    target, count_hbm, after, x_hbm, w_hbm, acc_ref, m0_ref, m1_ref,
+    xv, wv, st, sb, live, xsem, wsem, lsem,
 ):
     states = [
         pltpu.make_async_copy(x_hbm.at[:, :, pl.ds(256 * p, 256)], xv.at[p], xsem.at[p])
@@ -186,6 +187,8 @@
         states[p].start()
     for c in chunks.values():
         c.start()
+    counts = pltpu.make_async_copy(count_hbm, live, lsem)
+    counts.start()
     low, high = half_lanes()
     low = jnp.concatenate([low, low], axis=0)
     high = jnp.concatenate([high, high], axis=0)
@@ -203,6 +206,8 @@
             sb[128 * p + 8 * q : 128 * p + 8 * q + 8] = (
                 st[256 * q : 256 * q + 256].astype(BF16).reshape(8, 32, 128)
             )
+    counts.wait()
+    count = live[0, 0]
     for p in range(2):
         for c in range(4):
             for h in range(2):
@@ -220,7 +225,7 @@
                     if p == 0:
                         acc_ref[target[n]] = v
                     else:
-                        acc_ref[jnp.where(n < count[0], target[n], 256)] += v
+                        acc_ref[jnp.where(n < count, target[n], 256)] += v
     send_sides(m0_ref, m1_ref, lambda q: acc_ref[8 * q + 7], lambda q: acc_ref[8 * q])
 
 
@@ -229,7 +234,7 @@
     return pl.pallas_call(
         sums_kernel,
         name="inner_sums",
-        in_specs=[SMEM, SMEM, VMEM, HBM, HBM],
+        in_specs=[SMEM, HBM, VMEM, HBM, HBM],
         out_specs=[VMEM, VMEM, VMEM],
         out_shape=[pltpu.VMEM((257, 32, 128), F32), side, side],
         scratch_shapes=[
@@ -237,8 +242,10 @@
             pltpu.VMEM((512, 64, 128), BF16),
             pltpu.VMEM((4096, 128), F32),
             pltpu.VMEM((256, 32, 128), BF16),
+            pltpu.SMEM((1, 1), jnp.int32),
             pltpu.SemaphoreType.DMA((2,)),
             pltpu.SemaphoreType.DMA((2, 4, 2)),
+            pltpu.SemaphoreType.DMA,
         ],
         cost_estimate=pl.CostEstimate(
             flops=2 * 512 * 32 * 64 * 128, bytes_accessed=16 << 20, transcendentals=0
@@ -674,7 +681,7 @@
     rb0 = exchange(m0, LON_EVEN)
     rb1 = exchange(m1, LON_ODD)
     acc, i0, i1 = inner_sums(
-        block_target[0, 0], block_count[0], after, cell_state[0, 0], remap_weight[0, 0]
+        block_target[0, 0], block_count, after, cell_state[0, 0], remap_weight[0, 0]
     )
     ri0 = exchange(i0, LON_EVEN)
     ri1 = exchange(i1, LON_ODD)

time: 54.1 us -> 54.1 us (level)
  no operation moved by 1% of the time
where the time goes in v4:
time: 54.1 us; the launch traced here: 53.9 us
  Pallas kernels  33.2 us (61%)
  starting transfers between devices  13.3 us (25%)
  waiting for transfers between devices  6.63 us (12%)
  between operations  0.82 us (2%)
    ppermute x6, starting transfers between devices, exchange(): return lax.ppermute(block, ('lat', 'lon'), pairs)  13.3 us
    pallas_call x1, Pallas kernels, inner_sums(): pl.pallas_call(sums_kernel, name='inner_sums', in_specs=[SMEM, HBM, VMEM,...  10.8 us
    ppermute x6, waiting for transfers between devices, exchange(): return lax.ppermute(block, ('lat', 'lon'), pairs)  6.63 us
    pallas_call x1, Pallas kernels, first_conv(): pl.pallas_call(first_kernel, name='first_conv', in_specs=[VMEM] * 4, out_...  6.29 us
    pallas_call x1, Pallas kernels, second_conv(): pl.pallas_call(second_kernel, name='second_conv', in_specs=[VMEM] * 8, ou...  5.03 us
    pallas_call x1, Pallas kernels, build_interior(): pl.pallas_call(interior_kernel, name='build_interior', in_specs=[VMEM], o...  3.86 us
    pallas_call x1, Pallas kernels, build_field(): pl.pallas_call(field_kernel, name='build_field', in_specs=[VMEM] * 8, out...  3.38 us
    pallas_call x1, Pallas kernels, border_sums(): pl.pallas_call(border_kernel, name='border_sums', in_specs=[HBM, HBM, HBM...  2.96 us
  transfers between devices with their start and end apart: 6, of which 2 were waited for; matrix products, arithmetic and copies ran while one was open for 0% of the time, Pallas kernels for 20%

profile of v4, /device:TPU:1, one launch (start us, length us, event | category | flops | bytes accessed | tf_op | source)
XLA Modules:
  0.0 53.9 jit_solution(7533505943013846691)
XLA Ops:
  0.0 0.0 copy-start.2
  0.7 3.0 %border_sums.1 = (bf16[32,32,128]{2,1,0:T(8,128)(2,1)S(1)}, bf16[32,32,128]{2,1,0:T(8,128)(2,1)S(1)}, f32[8,128]{1,0:T(8,128)S(1)}) custom-call(s32[128]{0:T(128)} %bitcast.27, bf16[32,64,128]{2,1,0:T(8,128)(2,1)} %bitcast.26, bf16[128,64,128]{2,1,0:T(8,128)(2,1)} %bitcast.24), custom_call_target="tpu_custom_call" | custom-call | flops 67108864 | bytes 4194304 | tf_op jit(solution)/shard_map/border_sums/pallas_call | solution.py:146
  3.6 0.0 copy-done.2
  3.6 0.0 copy-start
  3.7 0.0 copy-start.1
  3.7 0.0 copy-start.3
  3.7 0.0 copy-start.4
  3.7 0.0 copy-start.5
  3.7 0.0 copy-start.6
  3.7 10.8 %inner_sums.1 = (f32[257,32,128]{2,1,0:T(8,128)S(1)}, bf16[32,32,128]{2,1,0:T(8,128)(2,1)S(1)}, bf16[32,32,128]{2,1,0:T(8,128)(2,1)S(1)}) custom-call(s32[512]{0:T(512)S(1)} %bitcast.18, s32[1,1]{1,0:T(1,128)S(6)} %copy.16.count_hbm, f32[8,128]{1,0:T(8,128)S(1)} %get-tuple-element.18.after, bf16[32,64,512]{2,1,0:T(8,128)(2,1)} %bitcast.25, ...), custom_call_target="tpu_custom_call" | custom-call | flops 268435456 | bytes 16777216 | tf_op jit(solution)/shard_map/inner_sums/pallas_call | solution.py:234
  14.5 2.2 %collective-permute-start.2 = (bf16[32,32,128]{2,1,0:T(8,128)(2,1)S(1)}, bf16[32,32,128]{2,1,0:T(8,128)(2,1)S(1)}, u32[]{:S(2)}, u32[]{:S(2)}) collective-permute-start(bf16[32,32,128]{2,1,0:T(8,128)(2,1)S(1)} %get-tuple-element.22), channel_id=1, source_target_pairs={{0,1},{1,0},{2,3},{3,2},{4,5},{5,4},{6,7},{7,6},{8,9},{9,8},{10,11... | collective-permute-start | bytes 786440 | tf_op jit(solution)/shard_map/ppermute | solution.py:32
  16.7 7.4 %collective-permute-start.3 = (bf16[32,32,128]{2,1,0:T(8,128)(2,1)S(1)}, bf16[32,32,128]{2,1,0:T(8,128)(2,1)S(1)}, u32[]{:S(2)}, u32[]{:S(2)}) collective-permute-start(bf16[32,32,128]{2,1,0:T(8,128)(2,1)S(1)} %get-tuple-element.23), channel_id=1, source_target_pairs={{0,31},{1,2},{2,1},{3,4},{4,3},{5,6},{6,5},{7,8},{8,7},{9,10},{10,... | collective-permute-start | bytes 786440 | tf_op jit(solution)/shard_map/ppermute | solution.py:32
  24.1 0.0 collective-permute-start
  24.1 0.9 %collective-permute-start.1 = (bf16[32,32,128]{2,1,0:T(8,128)(2,1)S(1)}, bf16[32,32,128]{2,1,0:T(8,128)(2,1)S(1)}, u32[]{:S(2)}, u32[]{:S(2)}) collective-permute-start(bf16[32,32,128]{2,1,0:T(8,128)(2,1)S(1)} %get-tuple-element.21.m1_ref), channel_id=1, source_target_pairs={{0,31},{1,2},{2,1},{3,4},{4,3},{5,6},{6,5},{7,8},{8,7},{9,10},{10,... | collective-permute-start | bytes 786440 | tf_op jit(solution)/shard_map/ppermute | solution.py:32
  25.0 0.0 copy-done
  25.0 0.0 copy-done.1
  25.0 0.0 copy-done.3
  25.1 0.0 copy-done.4
  25.1 0.0 copy-done.5
  25.1 0.0 copy-done.6
  25.1 0.8 %matrix_weights.1 = (bf16[3584,256]{1,0:T(8,128)(2,1)S(1)}, bf16[4480,256]{1,0:T(8,128)(2,1)S(1)}, f32[8,256]{1,0:T(8,128)S(1)}) custom-call(bf16[49,32,64]{2,1,0:T(8,128)(2,1)S(1)} %bitcast.17, bf16[49,64,128]{2,1,0:T(8,128)(2,1)S(1)} %bitcast.16, f32[1,64]{1,0:T(1,128)S(1)} %bitcast.19, f32[1,64]{1,0:T(1,128)S(1)} %bitcast.20, f32[1,128]{1,0:T(1,128)S(1)} %bitcast.21, ...), custom_call_target="tpu_custom_call" | custom-call | bytes 8388608 | tf_op jit(solution)/shard_map/matrix_weights/pallas_call | solution.py:277
  25.9 3.9 %build_interior.1.inside = bf16[4,132,2,16,128]{4,3,2,1,0:T(8,128)(2,1)S(1)} custom-call(f32[257,32,128]{2,1,0:T(8,128)S(1)} %get-tuple-element.19.acc), custom_call_target="tpu_custom_call" | custom-call | flops 268435456 | bytes 8388608 | tf_op jit(solution)/shard_map/build_interior/pallas_call | solution.py:341
  29.8 0.0 collective-permute-done.2.ri0_ref
  29.8 0.0 collective-permute-done.3.ri1_ref
  29.8 0.9 %collective-permute-done.rb0_ref = bf16[32,32,128]{2,1,0:T(8,128)(2,1)S(1)} collective-permute-done((bf16[32,32,128]{2,1,0:T(8,128)(2,1)S(1)}, bf16[32,32,128]{2,1,0:T(8,128)(2,1)S(1)}, u32[]{:S(2)}, u32[]{:S(2)}) %collective-permute-start) | collective-permute-done | bytes 262176 | tf_op jit(solution)/shard_map/ppermute | solution.py:32
  30.7 5.7 %collective-permute-done.1.rb1_ref = bf16[32,32,128]{2,1,0:T(8,128)(2,1)S(1)} collective-permute-done((bf16[32,32,128]{2,1,0:T(8,128)(2,1)S(1)}, bf16[32,32,128]{2,1,0:T(8,128)(2,1)S(1)}, u32[]{:S(2)}, u32[]{:S(2)}) %collective-permute-start.1) | collective-permute-done | bytes 262176 | tf_op jit(solution)/shard_map/ppermute | solution.py:32
  36.4 3.4 %build_field.1 = (bf16[4,132,2,16,128]{4,3,2,1,0:T(8,128)(2,1)S(1)}, f32[7,272,128]{2,1,0:T(8,128)S(1)}, bf16[5,5,2,16,128]{4,3,2,1,0:T(8,128)(2,1)S(1)}, bf16[5,5,2,16,128]{4,3,2,1,0:T(8,128)(2,1)S(1)}) custom-call(bf16[4,132,2,16,128]{4,3,2,1,0:T(8,128)(2,1)S(1)} %build_interior.1.inside, ...), custom_call_target="tpu_custom_call", output_to_operand_aliasing={{0}: (0, {})} | custom-call | tf_op jit(solution)/shard_map/build_field/pallas_call | solution.py:416
  39.8 2.8 %collective-permute-start.4 = (bf16[5,5,2,16,128]{4,3,2,1,0:T(8,128)(2,1)S(1)}, bf16[5,5,2,16,128]{4,3,2,1,0:T(8,128)(2,1)S(1)}, u32[]{:S(2)}, u32[]{:S(2)}) collective-permute-start(bf16[5,5,2,16,128]{4,3,2,1,0:T(8,128)(2,1)S(1)} %get-tuple-element.28.ma_ref), channel_id=1, source_target_pairs={{0,16},{1,17},{2,18},{3,19},{4,20},{5,21},{6,22},{7,23},{8,24},{9,... | collective-permute-start | bytes 614408 | tf_op jit(solution)/shard_map/ppermute | solution.py:32
  42.6 0.0 collective-permute-start.5
  42.6 6.3 %first_conv.1.h_ref = bf16[5,64,2,16,128]{4,3,2,1,0:T(8,128)(2,1)S(1)} custom-call(bf16[4,132,2,16,128]{4,3,2,1,0:T(8,128)(2,1)S(1)} %get-tuple-element.24.f_ref, f32[7,272,128]{2,1,0:T(8,128)S(1)} %get-tuple-element.25.e_ref, bf16[3584,256]{1,0:T(8,128)(2,1)S(1)} %get-tuple-element.26.w_ref.w1_ref, f32[8,256]{1,0:T(8,128)S(1)} %get-tuple-element.27.v_ref), custom_call_target="tpu_custom_call" | custom-call | flops 4227858432 | bytes 12582912 | tf_op jit(solution)/shard_map/first_conv/pallas_call | solution.py:504
  48.9 0.0 collective-permute-done.4.ra_ref
  48.9 0.0 collective-permute-done.5.rb_ref
  48.9 5.0 %second_conv.1 = bf16[64,32,128]{2,1,0:T(8,128)(2,1)} custom-call(bf16[5,64,2,16,128]{4,3,2,1,0:T(8,128)(2,1)S(1)} %first_conv.1.h_ref, bf16[5,5,2,16,128]{4,3,2,1,0:T(8,128)(2,1)S(1)} %get-tuple-element.28.ma_ref, bf16[5,5,2,16,128]{4,3,2,1,0:T(8,128)(2,1)S(1)} %get-tuple-element.29.mb_ref, bf16[5,5,2,16,128]{4,3,2,1,0:T(8,128)(2,1)S(1)} %collective-permute-done.4.ra_ref, ...), custom_call_target="tpu_custom_call" | custom-call | tf_op jit(solution)/shard_map/second_conv/pallas_call | solution.py:644
Async XLA Ops:
  0.0 3.6 %copy-start.2 = (s32[1,1,512]{2,1,0:T(1,128)S(1)}, s32[1,1,512]{2,1,0:T(1,128)}, u32[]{:S(2)}) copy-start(s32[1,1,512]{2,1,0:T(1,128)} %param.15) | copy-start | bytes 6148
  3.6 21.4 %copy-start = (bf16[7,7,64,128]{3,2,1,0:T(8,128)(2,1)S(1)}, bf16[7,7,64,128]{3,2,1,0:T(8,128)(2,1)}, u32[]{:S(2)}) copy-start(bf16[7,7,64,128]{3,2,1,0:T(8,128)(2,1)} %param.23) | copy-start | bytes 2408452
  3.7 21.4 %copy-start.1 = (bf16[7,7,32,64]{3,2,1,0:T(8,128)(2,1)S(1)}, bf16[7,7,32,64]{3,2,1,0:T(8,128)(2,1)}, u32[]{:S(2)}) copy-start(bf16[7,7,32,64]{3,2,1,0:T(8,128)(2,1)} %param.20) | copy-start | bytes 602116
  3.7 21.4 %copy-start.3 = (f32[64]{0:T(128)S(1)}, f32[64]{0:T(128)}, u32[]{:S(2)}) copy-start(f32[64]{0:T(128)} %param.21) | copy-start | bytes 772
  3.7 21.4 %copy-start.4 = (f32[64]{0:T(128)S(1)}, f32[64]{0:T(128)}, u32[]{:S(2)}) copy-start(f32[64]{0:T(128)} %param.22) | copy-start | bytes 772
  3.7 21.4 %copy-start.5 = (f32[128]{0:T(128)S(1)}, f32[128]{0:T(128)}, u32[]{:S(2)}) copy-start(f32[128]{0:T(128)} %param.24) | copy-start | bytes 1540
  3.7 21.4 %copy-start.6 = (f32[128]{0:T(128)S(1)}, f32[128]{0:T(128)}, u32[]{:S(2)}) copy-start(f32[128]{0:T(128)} %param.25) | copy-start | bytes 1540
  14.5 15.3 %collective-permute-start.2 = (bf16[32,32,128]{2,1,0:T(8,128)(2,1)S(1)}, bf16[32,32,128]{2,1,0:T(8,128)(2,1)S(1)}, u32[]{:S(2)}, u32[]{:S(2)}) collective-permute-start(bf16[32,32,128]{2,1,0:T(8,128)(2,1)S(1)} %get-tuple-element.22), channel_id=1, source_target_pairs={{0,1},{1,0},{2,3},{3,2},{4,5},{5,4},{6,7},{7,6},{8,9},{9,8},{10,11... | collective-permute-start | bytes 786440 | tf_op jit(solution)/shard_map/ppermute | solution.py:32
  16.7 13.1 %collective-permute-start.3 = (bf16[32,32,128]{2,1,0:T(8,128)(2,1)S(1)}, bf16[32,32,128]{2,1,0:T(8,128)(2,1)S(1)}, u32[]{:S(2)}, u32[]{:S(2)}) collective-permute-start(bf16[32,32,128]{2,1,0:T(8,128)(2,1)S(1)} %get-tuple-element.23), channel_id=1, source_target_pairs={{0,31},{1,2},{2,1},{3,4},{4,3},{5,6},{6,5},{7,8},{8,7},{9,10},{10,... | collective-permute-start | bytes 786440 | tf_op jit(solution)/shard_map/ppermute | solution.py:32
  24.1 6.6 %collective-permute-start = (bf16[32,32,128]{2,1,0:T(8,128)(2,1)S(1)}, bf16[32,32,128]{2,1,0:T(8,128)(2,1)S(1)}, u32[]{:S(2)}, u32[]{:S(2)}) collective-permute-start(bf16[32,32,128]{2,1,0:T(8,128)(2,1)S(1)} %get-tuple-element.20.m0_ref), channel_id=1, source_target_pairs={{0,1},{1,0},{2,3},{3,2},{4,5},{5,4},{6,7},{7,6},{8,9},{9,8},{10,11... | collective-permute-start | bytes 786440 | tf_op jit(solution)/shard_map/ppermute | solution.py:32
  24.1 12.3 %collective-permute-start.1 = (bf16[32,32,128]{2,1,0:T(8,128)(2,1)S(1)}, bf16[32,32,128]{2,1,0:T(8,128)(2,1)S(1)}, u32[]{:S(2)}, u32[]{:S(2)}) collective-permute-start(bf16[32,32,128]{2,1,0:T(8,128)(2,1)S(1)} %get-tuple-element.21.m1_ref), channel_id=1, source_target_pairs={{0,31},{1,2},{2,1},{3,4},{4,3},{5,6},{6,5},{7,8},{8,7},{9,10},{10,... | collective-permute-start | bytes 786440 | tf_op jit(solution)/shard_map/ppermute | solution.py:32
  39.8 9.1 %collective-permute-start.4 = (bf16[5,5,2,16,128]{4,3,2,1,0:T(8,128)(2,1)S(1)}, bf16[5,5,2,16,128]{4,3,2,1,0:T(8,128)(2,1)S(1)}, u32[]{:S(2)}, u32[]{:S(2)}) collective-permute-start(bf16[5,5,2,16,128]{4,3,2,1,0:T(8,128)(2,1)S(1)} %get-tuple-element.28.ma_ref), channel_id=1, source_target_pairs={{0,16},{1,17},{2,18},{3,19},{4,20},{5,21},{6,22},{7,23},{8,24},{9,... | collective-permute-start | bytes 614408 | tf_op jit(solution)/shard_map/ppermute | solution.py:32
  42.6 6.3 %collective-permute-start.5 = (bf16[5,5,2,16,128]{4,3,2,1,0:T(8,128)(2,1)S(1)}, bf16[5,5,2,16,128]{4,3,2,1,0:T(8,128)(2,1)S(1)}, u32[]{:S(2)}, u32[]{:S(2)}) collective-permute-start(bf16[5,5,2,16,128]{4,3,2,1,0:T(8,128)(2,1)S(1)} %get-tuple-element.29.mb_ref), channel_id=1, source_target_pairs={{0,32},{1,33},{2,34},{3,35},{4,36},{5,37},{6,38},{7,39},{8,40},{9,... | collective-permute-start | bytes 614408 | tf_op jit(solution)/shard_map/ppermute | solution.py:32
